TPU v7x, 128 devices: a whole 4x4x4 slice. The times are simulated.
128 devices in a mesh: dp: 16 (over y, z), tensor: 8 (over x, core).
Axes of the slice: x: 4, y: 4, z: 4, core: 2. Of those that a mesh axis runs over, the one named last changes fastest.
Arguments:
- prefill_rows: bfloat16 [8192, 2048], P(('dp', 'tensor')), may hold values from -6 to 6
- decode_rows: bfloat16 [256, 2048], P(('dp', 'tensor')), may hold values from -6 to 6
- deal_order: int32 [256], replicated, may hold values from 0 to 255, each once
- prefill_offset: int32 [16], P('dp'), may hold values from 0 to 1024, as said below
- cache_length: int32 [256], P('dp'), may hold values from 1 to 1024, as said below
- prefill_cache: bfloat16 [2, 16, 1024, 1024], P(None, 'dp', None, 'tensor'), may hold values from -480 to 480, as said below
- decode_cache: bfloat16 [2, 256, 1024, 1024], P(None, 'dp', None, 'tensor'), may hold values from -480 to 480, as said below
- qkv_weight: bfloat16 [2048, 8, 512], P(None, 'tensor'), may hold values from -0.125 to 0.125
- out_weight: bfloat16 [2048, 2048], P('tensor'), may hold values from -0.125 to 0.125
- attention_gain: float32 [2048], replicated, may hold values from 0.1 to 1.9
- forward_gain: float32 [2048], replicated, may hold values from 0.1 to 1.9
- gate_weight: bfloat16 [2048, 8192], P(None, 'tensor'), may hold values from -0.125 to 0.125
- up_weight: bfloat16 [2048, 8192], P(None, 'tensor'), may hold values from -0.125 to 0.125
- down_weight: bfloat16 [8192, 2048], P('tensor'), may hold values from -0.0625 to 0.0625
Outputs:
- prefill_out: bfloat16 [8192, 2048], P(('dp', 'tensor'))
- decode_out: bfloat16 [256, 2048], P(('dp', 'tensor'))
- prefill_entries: bfloat16 [2, 8192, 1024], P(None, 'dp', 'tensor')
- decode_entries: bfloat16 [2, 256, 1024], P(None, 'dp', 'tensor')
Inputs may be any that keep to these rules, and one draw needn't show every extreme that they name: A permutation: request r is held in slot deal_order[r]; slot s belongs to request group s // 16. `prefill_offset`: stored positions of each prefill request; some request has exactly 1024. `cache_length`: stored positions of the decode request in each slot; some slot has exactly 1024. `prefill_cache`: stored rotated keys and values; positions at or past a request's stored count hold unrelated numbers. `decode_cache`: stored rotated keys and values; positions at or past a slot's stored count hold unrelated numbers.
All inputs are finite; a program needn't handle non-finite values.
Results may differ from a plain program's by a relative error of at most 0.015.
The roundings to bfloat16 on the way count: a program that leaves them out, or rounds other values in their place, can miss the bound.
Values may be sent and summed in bfloat16 or wider, within the bound.
A program may use at most 128 MiB of HBM per device.

v0:
```python
import math

import jax
import jax.numpy as jnp
from jax import lax
from jax.sharding import PartitionSpec as P

HD = 128


EPSILON = 1e-06
THETA = 1000000.0
NEGATIVE = -1e30


def root_norm(rows, gain):
    values = rows.astype(jnp.float32)
    spread = jnp.mean(values * values, axis=-1, keepdims=True)
    return (values * lax.rsqrt(spread + EPSILON) * gain).astype(jnp.bfloat16)


def rotate(vectors, places):
    halfway = vectors.shape[-1] // 2
    powers = jnp.arange(halfway, dtype=jnp.float32) * (2.0 / vectors.shape[-1])
    inverse = THETA ** (-powers)
    angles = places.astype(jnp.float32)[:, None] * inverse[None, :]
    cosine = jnp.cos(angles)[:, None, :]
    sine_part = jnp.sin(angles)[:, None, :]
    leading = vectors[..., :halfway]
    trailing = vectors[..., halfway:]
    return jnp.concatenate(
        [leading * cosine - trailing * sine_part, trailing * cosine + leading * sine_part], axis=-1
    )


def project(normed, places, qkv_weight):
    heads = qkv_weight.shape[1]
    width = qkv_weight.shape[2]
    groups = width // HD - 2
    count = normed.shape[0]
    mixed = jnp.dot(
        normed,
        qkv_weight.reshape(qkv_weight.shape[0], heads * width),
        preferred_element_type=jnp.float32,
    )
    mixed = mixed.reshape(count, heads, groups + 2, HD)
    queries = rotate(mixed[:, :, :groups].reshape(count, heads * groups, HD), places)
    queries = queries.reshape(count, heads, groups, HD).astype(jnp.bfloat16)
    new_keys = rotate(mixed[:, :, groups], places).astype(jnp.bfloat16)
    new_values = mixed[:, :, groups + 1].astype(jnp.bfloat16)
    return (queries, new_keys, new_values)


def fill_attend(queries, new_keys, new_values, cache_keys, cache_values, offset):
    scaling = 1.0 / math.sqrt(HD)
    count = queries.shape[0]
    prior_count = cache_keys.shape[0]
    cached_scores = (
        jnp.einsum("qkgd,skd->kgqs", queries, cache_keys, preferred_element_type=jnp.float32)
        * scaling
    )
    fresh_scores = (
        jnp.einsum("qkgd,skd->kgqs", queries, new_keys, preferred_element_type=jnp.float32)
        * scaling
    )
    cached_allowed = jnp.arange(prior_count, dtype=jnp.int32)[None, :] < offset
    fresh_allowed = (
        jnp.arange(count, dtype=jnp.int32)[None, :] <= jnp.arange(count, dtype=jnp.int32)[:, None]
    )
    scores = jnp.concatenate(
        [
            jnp.where(cached_allowed, cached_scores, NEGATIVE),
            jnp.where(fresh_allowed, fresh_scores, NEGATIVE),
        ],
        axis=-1,
    )
    row_top = jnp.max(scores, axis=-1, keepdims=True)
    weights = jnp.exp(scores - row_top)
    weights = (weights / jnp.sum(weights, axis=-1, keepdims=True)).astype(jnp.bfloat16)
    attended = jnp.einsum(
        "kgqs,skd->qkgd",
        weights[..., :prior_count],
        cache_values,
        preferred_element_type=jnp.float32,
    )
    attended = attended + jnp.einsum(
        "kgqs,skd->qkgd", weights[..., prior_count:], new_values, preferred_element_type=jnp.float32
    )
    return attended.astype(jnp.bfloat16)


def step_attend(queries, new_keys, new_values, cache_keys, cache_values, lengths):
    scaling = 1.0 / math.sqrt(HD)
    stored = cache_keys.shape[1]
    cached_scores = (
        jnp.einsum("nkgd,nskd->nkgs", queries, cache_keys, preferred_element_type=jnp.float32)
        * scaling
    )
    own_scores = (
        jnp.einsum("nkgd,nkd->nkg", queries, new_keys, preferred_element_type=jnp.float32)[
            ..., None
        ]
        * scaling
    )
    allowed = (jnp.arange(stored, dtype=jnp.int32)[None, :] < lengths[:, None])[:, None, None, :]
    scores = jnp.concatenate([jnp.where(allowed, cached_scores, NEGATIVE), own_scores], axis=-1)
    row_top = jnp.max(scores, axis=-1, keepdims=True)
    weights = jnp.exp(scores - row_top)
    weights = (weights / jnp.sum(weights, axis=-1, keepdims=True)).astype(jnp.bfloat16)
    attended = jnp.einsum(
        "nkgs,nskd->nkgd", weights[..., :stored], cache_values, preferred_element_type=jnp.float32
    )
    attended = (
        attended
        + weights[..., stored:].astype(jnp.float32) * new_values.astype(jnp.float32)[:, :, None, :]
    )
    return attended.astype(jnp.bfloat16)


def feed_forward(inner, gate_weight, up_weight, down_weight):
    gate_part = jnp.dot(inner, gate_weight, preferred_element_type=jnp.float32)
    up_part = jnp.dot(inner, up_weight, preferred_element_type=jnp.float32)
    hidden = (jax.nn.silu(gate_part) * up_part).astype(jnp.bfloat16)
    return jnp.dot(hidden, down_weight, preferred_element_type=jnp.float32)


def on_device(
    prefill_rows,
    decode_rows,
    deal_order,
    prefill_offset,
    cache_length,
    prefill_cache,
    decode_cache,
    qkv_weight,
    out_weight,
    attention_gain,
    forward_gain,
    gate_weight,
    up_weight,
    down_weight,
):
    tensor_count = lax.axis_size("tensor")
    tensor_place = lax.axis_index("tensor")
    group_place = lax.axis_index("dp")
    per_device = decode_rows.shape[0]
    share_rows = prefill_rows.shape[0]
    everyone = lax.all_gather(decode_rows, ("dp", "tensor"), axis=0, tiled=True)
    first_slot = (group_place * tensor_count + tensor_place) * per_device
    my_slots = first_slot + jnp.arange(per_device, dtype=jnp.int32)
    chooser = (deal_order[None, :] == my_slots[:, None]).astype(jnp.bfloat16)
    dealt = jnp.dot(chooser, everyone, preferred_element_type=jnp.float32).astype(jnp.bfloat16)
    fill_raw, step_raw = (
        lax.all_gather(prefill_rows, "tensor", axis=0, tiled=True),
        lax.all_gather(dealt, "tensor", axis=0, tiled=True),
    )
    fill_normed = root_norm(fill_raw, attention_gain)
    step_normed = root_norm(step_raw, attention_gain)
    total_tokens = fill_normed.shape[0]
    slot_group = step_normed.shape[0]
    local_heads = qkv_weight.shape[1]
    fill_places = prefill_offset[0] + jnp.arange(total_tokens, dtype=jnp.int32)
    fill_query, fill_keys, fill_values = project(fill_normed, fill_places, qkv_weight)
    step_query, step_keys, step_values = project(step_normed, cache_length, qkv_weight)
    prior_count = prefill_cache.shape[2]
    fill_att = fill_attend(
        fill_query,
        fill_keys,
        fill_values,
        prefill_cache[0, 0].reshape(prior_count, local_heads, HD),
        prefill_cache[1, 0].reshape(prior_count, local_heads, HD),
        prefill_offset[0],
    )
    stored = decode_cache.shape[2]
    step_att = step_attend(
        step_query,
        step_keys,
        step_values,
        decode_cache[0].reshape(slot_group, stored, local_heads, HD),
        decode_cache[1].reshape(slot_group, stored, local_heads, HD),
        cache_length,
    )
    fill_part = jnp.dot(
        fill_att.reshape(total_tokens, -1), out_weight, preferred_element_type=jnp.float32
    )
    step_part = jnp.dot(
        step_att.reshape(slot_group, -1), out_weight, preferred_element_type=jnp.float32
    )
    fill_sum, step_sum = lax.psum((fill_part, step_part), "tensor")
    fill_resid = (fill_raw.astype(jnp.float32) + fill_sum).astype(jnp.bfloat16)
    step_resid = (step_raw.astype(jnp.float32) + step_sum).astype(jnp.bfloat16)
    fill_inner = root_norm(fill_resid, forward_gain)
    step_inner = root_norm(step_resid, forward_gain)
    fill_keep = lax.dynamic_slice_in_dim(fill_resid, tensor_place * share_rows, share_rows, 0)
    step_keep = lax.dynamic_slice_in_dim(step_resid, tensor_place * per_device, per_device, 0)
    fill_more = feed_forward(fill_inner, gate_weight, up_weight, down_weight)
    step_more = feed_forward(step_inner, gate_weight, up_weight, down_weight)
    fill_add, step_add = (
        lax.psum_scatter(
            fill_more.astype(jnp.bfloat16), "tensor", scatter_dimension=0, tiled=True
        ).astype(jnp.float32),
        lax.psum_scatter(
            step_more.astype(jnp.bfloat16), "tensor", scatter_dimension=0, tiled=True
        ).astype(jnp.float32),
    )
    prefill_out = (fill_keep.astype(jnp.float32) + fill_add).astype(jnp.bfloat16)
    step_final = (step_keep.astype(jnp.float32) + step_add).astype(jnp.bfloat16)
    every_slot = lax.all_gather(step_final, ("dp", "tensor"), axis=0, tiled=True)
    wanted = lax.dynamic_slice_in_dim(deal_order, first_slot, per_device, 0)
    picker = (wanted[:, None] == jnp.arange(every_slot.shape[0], dtype=jnp.int32)[None, :]).astype(
        jnp.bfloat16
    )
    decode_out = jnp.dot(picker, every_slot, preferred_element_type=jnp.float32).astype(
        jnp.bfloat16
    )
    prefill_entries = jnp.stack(
        [
            fill_keys.reshape(total_tokens, local_heads * HD),
            fill_values.reshape(total_tokens, local_heads * HD),
        ]
    )
    decode_entries = jnp.stack(
        [
            step_keys.reshape(slot_group, local_heads * HD),
            step_values.reshape(slot_group, local_heads * HD),
        ]
    )
    return (prefill_out, decode_out, prefill_entries, decode_entries)


def solution(mesh):
    placed = (
        P(("dp", "tensor"), None),
        P(("dp", "tensor"), None),
        P(),
        P("dp"),
        P("dp"),
        P(None, "dp", None, "tensor"),
        P(None, "dp", None, "tensor"),
        P(None, "tensor", None),
        P("tensor", None),
        P(),
        P(),
        P(None, "tensor"),
        P(None, "tensor"),
        P("tensor", None),
    )
    return jax.shard_map(
        on_device,
        mesh=mesh,
        in_specs=placed,
        out_specs=(
            P(("dp", "tensor"), None),
            P(("dp", "tensor"), None),
            P(None, "dp", "tensor"),
            P(None, "dp", "tensor"),
        ),
        check_vma=False,
    )
```

profile of v0, /device:TPU:1, one launch (start us, length us, event | category | flops | bytes accessed | tf_op | source)
XLA Modules:
  0.0 375.1 jit_solution(13322457662285724771)
XLA Ops:
  7.2 0.7 all-gather.9.cloned.1.call-update
  8.0 0.7 all-gather.7.cloned.1.call-update
  8.8 0.7 convert_element_type.210
  9.4 1.3 iota_compare_fusion.1
  10.7 0.8 iota_compare_fusion
  11.5 2.9 copy.87
  15.1 0.1 multiply_cosine_fusion.3
  15.3 0.5 multiply_cosine_fusion.1
  15.8 0.6 iota_compare_fusion.2
  16.4 61.6 %all-gather.9.cloned.1.call-done = bf16[128,2,2048]{2,1,0:T(2,128)(2,1)} async-done(((bf16[1,2,2048]{2,1,0:T(2,128)(2,1)}), bf16[128,2,2048]{2,1,0:T(2,128)(2,1)}) %all-gather.9.cloned.1.call-update) | async-done | bytes 1048592 | tf_op jit(solution)/shard_map/all_gather | solution.py:148
  78.0 2.3 reshape.670
  80.3 1.5 fusion.16
  81.8 14.0 %all-gather.1 = bf16[8,2,2048]{2,1,0:T(2,128)(2,1)} all-gather(bf16[1,2,2048]{2,1,0:T(2,128)(2,1)S(1)} %fusion.16), channel_id=1, replica_groups=mesh['dp'=16,'tensor'=8] {'tensor'}, dimensions={0}, use_global_device_ids=true | all-gather | bytes 73728 | tf_op jit(solution)/shard_map/all_gather | solution.py:155
  95.7 0.9 reshape.675
  96.6 0.1 multiply_reduce_fusion
  96.7 1.3 convolution_bitcast_fusion
  98.1 0.8 fusion.87
  98.9 0.6 copy-done.11
  99.6 0.1 subtract_convert_fusion.1
  99.8 0.1 fusion.94
  99.9 4.1 %fusion.112 = (f32[16,2]{1,0:T(8,128)S(1)}, f32[16,2,1024]{2,1,0:T(2,128)}) fusion(bf16[2,16,1024,128]{3,2,1,0:T(8,128)(2,1)} %param.20, bf16[16,2,128]{2,0,1:T(8,128)(2,1)S(1)} %pad_maximum_fusion.4, pred[16,1024]{1,0:T(8,128)(4,1)} %iota_compare_fusion.1), kind=kOutput, calls=%fused_computation.159 | convolution fusion | flops 8486880 | bytes 4350080 | tf_op jit(solution)/shard_map/nkgd,nskd->nkgs/dot_general | solution.py:96
  103.9 0.6 multiply_maximum_fusion
  104.6 0.9 copy.69
  105.4 1.3 copy.91
  106.8 0.9 copy.68
  107.7 0.9 fusion.64
  108.6 0.8 divide_convert_fusion.1
  109.4 0.6 slice.103
  110.0 0.6 copy.96
  110.7 1.4 copy.76
  112.0 0.7 fusion.101
  112.7 2.8 fusion.38
  115.6 0.9 fusion.91
  116.5 2.1 fusion.5
  118.6 3.0 fusion.23
  121.8 0.6 fusion.58
  122.3 0.1 subtract_convert_fusion
  122.5 0.9 fusion.110
  123.3 0.7 fusion.111
  124.1 1.1 fusion.1
  125.2 1.2 divide_convert_fusion
  126.4 0.8 fusion.26
  127.2 0.5 fusion.27
  127.7 2.7 fusion.113
  130.5 0.2 all-reduce.5.cloned.1.call-start
  130.7 0.6 dynamic-slice
  132.0 66.7 %all-reduce.7.cloned.1.call-done = (f32[512,2048]{1,0:T(8,128)}, f32[16,2048]{1,0:T(8,128)}) async-done(((f32[512,2048]{1,0:T(8,128)}, f32[16,2048]{1,0:T(8,128)}), (f32[512,2048]{1,0:T(8,128)}, f32[16,2048]{1,0:T(8,128)})) %all-reduce.7.cloned.1.call-update) | async-done | bytes 4325392 | tf_op jit(solution)/shard_map/psum | solution.py:189
  198.7 1.0 fusion.54
  199.7 2.9 fusion.80
  202.6 5.5 %convolution_convert_fusion.1 = bf16[16,2048]{1,0:T(8,128)(2,1)} fusion(bf16[1024,2048]{1,0:T(8,128)(2,1)} %param.27, bf16[2048,1024]{1,0:T(8,128)(2,1)} %param.26, f32[16,1024]{1,0:T(8,128)S(1)} %fusion.80, bf16[16,2048]{1,0:T(8,128)(2,1)S(1)} %get-tuple-element.23, f32[2048]{0:T(1024)S(1)} %copy-done.15, f32[16]{0:T(128)S(1)} %add_rsqrt_fusion.2), kind=kOutput, calls=%fused_computation.25 | convolution fusion | flops 134479872 | bytes 8593472 | tf_op jit(solution)/shard_map/dot_general | solution.py:124
  208.2 4.1 %fusion.2 = (f32[512]{0:T(512)S(1)}, bf16[512,2048]{1,0:T(8,128)(2,1)}) fusion(f32[512,2048]{1,0:T(8,128)} %get-tuple-element.20, bf16[512,2048]{1,0:T(8,128)(2,1)S(1)} %copy-done.1), kind=kLoop, calls=%fused_computation.9 | loop fusion | flops 6290944 | bytes 8390656 | tf_op jit(solution)/shard_map/reduce_sum | solution.py:18
  212.3 55.2 %all-reduce.5.cloned.1.call-done = bf16[16,2048]{1,0:T(8,128)(2,1)} async-done(((bf16[16,2048]{1,0:T(8,128)(2,1)}), bf16[16,2048]{1,0:T(8,128)(2,1)}) %all-reduce.5.cloned.1.call-update) | async-done | bytes 65552
  267.5 1.4 fusion.90
  269.0 6.6 %fusion.43 = f32[512,1024]{1,0:T(8,128)} fusion(bf16[2048,1024]{1,0:T(8,128)(2,1)} %param.25, bf16[512,2048]{1,0:T(8,128)(2,1)} %get-tuple-element.25, f32[2048]{0:T(1024)S(1)} %copy-done.15, f32[512]{0:T(512)S(1)} %add_rsqrt_fusion), kind=kOutput, calls=%fused_computation.50 | convolution fusion | flops 2151677952 | bytes 8398848 | tf_op jit(solution)/shard_map/dot_general | solution.py:121
  275.7 10.0 %convolution_convert_fusion = bf16[512,2048]{1,0:T(8,128)(2,1)} fusion(bf16[1024,2048]{1,0:T(8,128)(2,1)} %param.27, f32[512,1024]{1,0:T(8,128)} %fusion.43, bf16[2048,1024]{1,0:T(8,128)(2,1)} %param.26, bf16[512,2048]{1,0:T(8,128)(2,1)S(1)} %copy-done.2, f32[2048]{0:T(1024)S(1)} %copy-done.15, f32[512]{0:T(512)S(1)} %add_rsqrt_fusion), kind=kOutput, calls=%fused_computation.24 | convolution fusion | flops 4303355904 | bytes 14690304 | tf_op jit(solution)/shard_map/dot_general | solution.py:124
  285.7 0.1 dynamic_slice.10
  285.8 0.7 pad_maximum_fusion.5
  286.5 1.0 fusion.76
  287.5 0.8 copy.77
  288.3 47.6 %all-gather.11.cloned.1.call-done = bf16[128,2,2048]{2,1,0:T(2,128)(2,1)} async-done(((bf16[1,2,2048]{2,1,0:T(2,128)(2,1)}), bf16[128,2,2048]{2,1,0:T(2,128)(2,1)}) %all-gather.11.cloned.1.call-update) | async-done | bytes 1048592 | tf_op jit(solution)/shard_map/all_gather | solution.py:208
  336.0 1.5 reshape.674
  337.5 0.9 convolution_convert_fusion.2
  338.3 28.1 %reduce-scatter.2.cloned.1.call-done = bf16[64,2048]{1,0:T(8,128)(2,1)} async-done(((bf16[512,2048]{1,0:T(8,128)(2,1)}), bf16[64,2048]{1,0:T(8,128)(2,1)}) %reduce-scatter.2.cloned.1.call-update) | async-done | bytes 262160 | tf_op jit(solution)/shard_map/reduce_scatter | solution.py:199
  366.4 1.8 add_convert_fusion
  (77 shorter events, 0.7 us)
Async XLA Ops:
  7.2 108.4 %copy-start = (bf16[256,2048]{1,0:T(8,128)(2,1)S(1)}, bf16[256,2048]{1,0:T(8,128)(2,1)}, u32[]{:S(2)}) copy-start(bf16[256,2048]{1,0:T(8,128)(2,1)} %param.22) | copy-start | bytes 3145732
  7.2 73.1 %copy-start.22 = (s32[256]{0:T(256)S(1)}, s32[256]{0:T(256)}, u32[]{:S(2)}) copy-start(s32[256]{0:T(256)} %param.16) | copy-start | bytes 3076
  7.2 70.8 %all-gather.9.cloned.1.call-start = ((), (), s32[]{:S(2)}) async-start(), calls=%async_computation.3 | async-start | bytes 1056768 | tf_op jit(solution)/shard_map/all_gather | solution.py:148
  7.9 108.6 %all-gather.7.cloned.1.call-start = ((), (), s32[]{:S(2)}) async-start(), calls=%async_computation.1 | async-start | bytes 2359296 | tf_op jit(solution)/shard_map/all_gather | solution.py:154
  8.7 190.0 %all-reduce.7.cloned.1.call-start = ((), (), s32[]{:S(2)}) async-start(), calls=%async_computation.6 | async-start | bytes 8650752 | tf_op jit(solution)/shard_map/psum | solution.py:189
  8.7 69.3 %copy-start.19 = (f32[64]{0:T(128)}, f32[64]{0:T(128)S(1)}, u32[]{:S(2)}) copy-start(f32[64]{0:T(128)S(1)} %negate_power_fusion) | copy-start | bytes 772
  9.4 72.4 %copy-start.21 = (f32[16]{0:T(128)}, f32[16]{0:T(128)S(1)}, u32[]{:S(2)}) copy-start(f32[16]{0:T(128)S(1)} %convert_element_type.210) | copy-start | bytes 196
  15.1 62.9 %copy-start.16 = (f32[512]{0:T(512)}, f32[512]{0:T(512)S(1)}, u32[]{:S(2)}) copy-start(f32[512]{0:T(512)S(1)} %add_convert_fusion.5) | copy-start | bytes 6148
  98.1 1.6 copy-start.10
  98.9 0.6 copy-start.11
  98.9 0.6 copy-start.13
  110.7 7.9 %copy-start.18 = (f32[2048]{0:T(1024)S(1)}, f32[2048]{0:T(1024)}, u32[]{:S(2)}) copy-start(f32[2048]{0:T(1024)} %param.23) | copy-start | bytes 24580
  118.6 3.1 copy-start.17
  118.6 3.1 copy-start.20
  118.6 3.8 %copy-start.9 = (bf16[2,1,1024,128]{3,2,1,0:T(8,128)(2,1)S(1)}, bf16[2,1,1024,128]{3,2,1,0:T(8,128)(2,1)}, u32[]{:S(2)}) copy-start(bf16[2,1,1024,128]{3,2,1,0:T(8,128)(2,1)} %param.19) | copy-start | bytes 1572868
  118.6 3.8 %copy-start.24 = (pred[1024]{0:T(1024)(128)(4,1)S(1)}, pred[1024]{0:T(1024)(128)(4,1)}, u32[]{:S(2)}) copy-start(pred[1024]{0:T(1024)(128)(4,1)} %iota_compare_fusion.2) | copy-start | bytes 3076
  121.6 5.6 %copy-start.3 = (f32[512,1,4,128]{0,3,2,1:T(8,128)}, f32[512,1,4,128]{0,3,2,1:T(8,128)S(1)}, u32[]{:S(2)}) copy-start(f32[512,1,4,128]{0,3,2,1:T(8,128)S(1)} %fusion.23) | copy-start | bytes 3145732
  121.7 1.7 copy-start.4
  122.3 1.7 copy-start.5
  122.3 1.7 copy-start.7
  127.7 3.0 copy-start.25
  130.5 69.2 %copy-start.15 = (f32[2048]{0:T(1024)S(1)}, f32[2048]{0:T(1024)}, u32[]{:S(2)}) copy-start(f32[2048]{0:T(1024)} %param.24) | copy-start | bytes 24580
  130.5 137.0 %all-reduce.5.cloned.1.call-start = ((), (), s32[]{:S(2)}) async-start(), calls=%async_computation.5 | async-start | bytes 131072
  202.6 5.6 %copy-start.1 = (bf16[512,2048]{1,0:T(8,128)(2,1)S(1)}, bf16[512,2048]{1,0:T(8,128)(2,1)}, u32[]{:S(2)}) copy-start(bf16[512,2048]{1,0:T(8,128)(2,1)} %all-gather.7.cloned.1.call-done) | copy-start | bytes 6291460
  208.1 127.9 %all-gather.11.cloned.1.call-start = ((), (), s32[]{:S(2)}) async-start(), calls=%async_computation.4 | async-start | bytes 1056768 | tf_op jit(solution)/shard_map/all_gather | solution.py:208
  268.9 97.5 %reduce-scatter.2.cloned.1.call-start = ((), (), s32[]{:S(2)}) async-start(), calls=%async_computation.2 | async-start | bytes 2359296 | tf_op jit(solution)/shard_map/reduce_scatter | solution.py:199
  269.0 6.7 %copy-start.2 = (bf16[512,2048]{1,0:T(8,128)(2,1)S(1)}, bf16[512,2048]{1,0:T(8,128)(2,1)}, u32[]{:S(2)}) copy-start(bf16[512,2048]{1,0:T(8,128)(2,1)} %get-tuple-element.25) | copy-start | bytes 6291460
  275.6 10.1 %copy-start.23 = (s32[256]{0:T(256)S(1)}, s32[256]{0:T(256)}, u32[]{:S(2)}) copy-start(s32[256]{0:T(256)} %param.16) | copy-start | bytes 3076
  275.6 10.2 %copy-start.12 = (bf16[16,1,64]{2,0,1:T(8,128)(2,1)S(1)}, bf16[16,1,64]{2,0,1:T(8,128)(2,1)}, u32[]{:S(2)}) copy-start(bf16[16,1,64]{2,0,1:T(8,128)(2,1)} %copy-done.11) | copy-start | bytes 6148
  275.6 10.2 %copy-start.14 = (bf16[16,1,64]{2,0,1:T(8,128)(2,1)S(1)}, bf16[16,1,64]{2,0,1:T(8,128)(2,1)}, u32[]{:S(2)}) copy-start(bf16[16,1,64]{2,0,1:T(8,128)(2,1)} %copy-done.13) | copy-start | bytes 6148
  275.6 11.8 %copy-start.6 = (bf16[512,1,64]{0,2,1:T(8,128)(2,1)S(1)}, bf16[512,1,64]{0,2,1:T(8,128)(2,1)}, u32[]{:S(2)}) copy-start(bf16[512,1,64]{0,2,1:T(8,128)(2,1)} %copy-done.5) | copy-start | bytes 196612
  275.7 11.8 %copy-start.8 = (bf16[512,1,64]{0,2,1:T(8,128)(2,1)S(1)}, bf16[512,1,64]{0,2,1:T(8,128)(2,1)}, u32[]{:S(2)}) copy-start(bf16[512,1,64]{0,2,1:T(8,128)(2,1)} %copy-done.7) | copy-start | bytes 196612
Sparse Core Ops, SparseCore 0:
  10.8 67.1 all-gather.8
  79.7 22.7 all-gather.6
  130.6 68.0 all-reduce.6
  208.2 59.2 all-reduce.4
  270.7 65.2 all-gather.10
  338.2 28.1 reduce-scatter.1
where the time goes:
time: 378 us; the launch traced here: 375 us
  waiting for transfers between devices  261 us (69%)
  matrix products  45.3 us (12%)
  other arithmetic  22.3 us (6%)
  local copies, waits for them, and re-layouts  16.6 us (4%)
  between operations  15.8 us (4%)
  blocking collectives  14 us (4%)
    psum x1, waiting for transfers between devices, on_device(): fill_sum, step_sum = lax.psum((fill_part, step_part), 'tensor')  66.7 us
    all_gather x1, waiting for transfers between devices, on_device(): everyone = lax.all_gather(decode_rows, ('dp', 'tensor'), axis=0, tiled=True)  61.6 us
    unnamed x7, waiting for transfers between devices  56.7 us
    all_gather x1, waiting for transfers between devices, on_device(): lax.all_gather(step_final, ('dp', 'tensor'), axis=0, tiled=True)  47.6 us
    reduce_scatter x1, waiting for transfers between devices, on_device(): lax.psum_scatter(fill_more.astype(jnp.bfloat16), 'tensor', scatter_dimens...  28.1 us
    dot_general x2, matrix products, feed_forward(): return jnp.dot(hidden, down_weight, preferred_element_type=jnp.float32)  15.5 us
    all_gather x1, blocking collectives, on_device(): lax.all_gather(dealt, 'tensor', axis=0, tiled=True)  14 us
    dot_general x2, matrix products, feed_forward(): gate_part = jnp.dot(inner, gate_weight, preferred_element_type=jnp.float32)  9.52 us
  transfers between devices with their start and end apart: 6, of which 5 were waited for; matrix products, arithmetic and copies ran while one was open for 15% of the time, Pallas kernels for 0%

commit v1 on v0

v1 whole, which is shorter than its diff:
```python
import functools
import math

import jax
import jax.numpy as jnp
from jax import lax
from jax.experimental import pallas as pl
from jax.experimental.pallas import tpu as pltpu
from jax.sharding import PartitionSpec as P

HD = 128
EPSILON = 1e-06
THETA = 1000000.0
NEGATIVE = -1e30
MESH = pl.DeviceIdType.MESH
F32 = jnp.float32
BF16 = jnp.bfloat16
NT = (((1,), (1,)), ((), ()))
HALF = 32
CHUNKS = 4


def normed(values, gain):
    spread = jnp.mean(values * values, axis=-1, keepdims=True)
    return (values * lax.rsqrt(spread + EPSILON) * gain).astype(BF16)


def layer_kernel(
    groups,
    rows_ref,
    drows_ref,
    deal_ref,
    off_ref,
    len_ref,
    cos_ref,
    sin_ref,
    again_ref,
    fgain_ref,
    pcache,
    dcache,
    qkv_hbm,
    out_hbm,
    gate_hbm,
    up_hbm,
    down_hbm,
    pout_ref,
    dout_ref,
    pent_ref,
    dent_ref,
    w_qkv,
    w_out,
    w_gate,
    w_up,
    w_down,
    kall,
    vall,
    kdec,
    vdec,
    xg1,
    xg2,
    mixed,
    qb,
    att,
    pb,
    rcv,
    cb,
    fb,
    nb,
    resid,
    hid,
    dpart,
    drs,
    dpb,
    dag,
    dsc,
    dpr,
    qpad,
    knew,
    vnew,
    dob,
    wsem,
    ags,
    agr,
    rss,
    rsr,
    crs,
    crr,
    dps,
    dpr_sem,
    cas,
    car,
):
    g = lax.axis_index("dp")
    t = lax.axis_index("tensor")
    x = t // 2
    c = t % 2
    width = rows_ref.shape[1]
    cw = width // CHUNKS
    bw = width // 8
    stored = pcache.shape[2]
    fresh = pent_ref.shape[1]
    slots = dent_ref.shape[1]
    dstored = dcache.shape[2]
    units = w_gate.shape[1]
    nreq = groups * slots
    scale2 = (1.0 / math.sqrt(HD)) * math.log2(math.e)

    partner = (g, t + 1 - 2 * c)
    right = (g, ((x + 1) % 4) * 2 + c)
    left = (g, ((x + 3) % 4) * 2 + c)
    sends = []

    def remote(src, dst, ss, rs, dev):
        copy = pltpu.make_async_remote_copy(
            src_ref=src, dst_ref=dst, send_sem=ss, recv_sem=rs, device_id=dev, device_id_type=MESH
        )
        copy.start()
        sends.append(copy)

    def arrived(dst, ss, rs):
        pltpu.make_async_remote_copy(
            src_ref=dst, dst_ref=dst, send_sem=ss, recv_sem=rs, device_id=partner, device_id_type=MESH
        ).wait_recv()

    local = {}

    def fetch(name, index, src, dst):
        copy = pltpu.make_async_copy(src, dst, wsem.at[index])
        copy.start()
        local[name] = copy

    fetch("qkv", 0, qkv_hbm, w_qkv)
    fetch("pk", 1, pcache.at[0, 0], kall.at[pl.ds(0, stored)])
    fetch("pv", 2, pcache.at[1, 0], vall.at[pl.ds(0, stored)])
    fetch("out", 3, out_hbm, w_out)
    fetch("dk", 4, dcache.at[0], kdec)
    fetch("dv", 5, dcache.at[1], vdec)
    fetch("gate", 6, gate_hbm, w_gate)
    fetch("up", 7, up_hbm, w_up)
    fetch("down", 8, down_hbm, w_down)

    barrier = pltpu.get_barrier_semaphore()
    for k in range(1, 8):
        pl.semaphore_signal(barrier, inc=1, device_id=(g, (t + k) % 8), device_id_type=MESH)
    for k in range(1, groups):
        pl.semaphore_signal(barrier, inc=1, device_id=((g + k) % groups, t), device_id_type=MESH)

    def buffer_of(stage, h):
        return (xg1 if stage == 0 else xg2).at[h]

    def ag_block(stage, h, b, p):
        return buffer_of(stage, h).at[pl.ds(HALF * b + 16 * p, 16)]

    def ag_send(stage, h, src_b, dst_b, p, number, dev):
        remote(
            ag_block(stage, h, src_b, p),
            ag_block(stage, h, dst_b, p),
            ags.at[stage, h, number],
            agr.at[stage, h, number],
            dev,
        )

    def ag_wait(stage, h, b, p, number):
        arrived(ag_block(stage, h, b, p), ags.at[stage, h, number], agr.at[stage, h, number])

    def ag_start(stage, h):
        ag_send(stage, h, 0, 6, 0, 1, right)
        ag_send(stage, h, 0, 2, 1, 4, left)
        ag_send(stage, h, 0, 6, 1, 2, right)
        ag_send(stage, h, 0, 2, 0, 3, left)
        ag_send(stage, h, 0, 1, 0, 0, partner)
        ag_send(stage, h, 0, 1, 1, 13, partner)

    def ag_forward(stage, h):
        ag_wait(stage, h, 6, 0, 1)
        ag_send(stage, h, 6, 4, 0, 5, right)
        ag_wait(stage, h, 2, 1, 4)
        ag_send(stage, h, 2, 4, 1, 6, left)
        ag_send(stage, h, 6, 7, 0, 7, partner)
        ag_send(stage, h, 2, 3, 1, 10, partner)
        ag_wait(stage, h, 6, 1, 2)
        ag_send(stage, h, 6, 7, 1, 8, partner)
        ag_wait(stage, h, 2, 0, 3)
        ag_send(stage, h, 2, 3, 0, 9, partner)

    def ag_far(stage, h):
        ag_wait(stage, h, 4, 0, 5)
        ag_send(stage, h, 4, 5, 0, 11, partner)
        ag_wait(stage, h, 4, 1, 6)
        ag_send(stage, h, 4, 5, 1, 12, partner)

    def ag_finish(stage, h):
        for b, p, number in (
            (1, 0, 0),
            (1, 1, 13),
            (7, 0, 7),
            (3, 1, 10),
            (7, 1, 8),
            (3, 0, 9),
            (5, 0, 11),
            (5, 1, 12),
        ):
            ag_wait(stage, h, b, p, number)

    def rs_split(stage, h, n, part):
        for b in range(8):
            pb[stage, h, n, b % 2, b // 2] = part[HALF * b : HALF * (b + 1)].astype(BF16)
        remote(
            pb.at[stage, h, n, 1],
            rcv.at[stage, h, n],
            rss.at[stage, h, n, 0],
            rsr.at[stage, h, n, 0],
            partner,
        )

    def on_chip(stage, h, n, d):
        return pb[stage, h, n, 0, d].astype(F32) + rcv[stage, h, n, d].astype(F32)

    def to_side(stage, h, n, d):
        side, dev = (0, right) if d == 1 else (1, left)
        remote(
            cb.at[stage, h, n, d],
            nb.at[stage, h, n, side],
            rss.at[stage, h, n, 2 + side],
            rsr.at[stage, h, n, 2 + side],
            dev,
        )

    def rs_combine(stage, h, n):
        arrived(rcv.at[stage, h, n], rss.at[stage, h, n, 0], rsr.at[stage, h, n, 0])
        cb[stage, h, n, 2] = on_chip(stage, h, n, 2).astype(BF16)
        remote(
            cb.at[stage, h, n, 2],
            fb.at[stage, h, n],
            rss.at[stage, h, n, 1],
            rsr.at[stage, h, n, 1],
            right if n % 2 == 0 else left,
        )
        d = 3 if n % 2 == 0 else 1
        cb[stage, h, n, d] = on_chip(stage, h, n, d).astype(BF16)
        to_side(stage, h, n, d)

    def rs_relay(stage, h, n):
        arrived(fb.at[stage, h, n], rss.at[stage, h, n, 1], rsr.at[stage, h, n, 1])
        d = 1 if n % 2 == 0 else 3
        cb[stage, h, n, d] = (on_chip(stage, h, n, d) + fb[stage, h, n].astype(F32)).astype(BF16)
        to_side(stage, h, n, d)

    def rs_total(stage, h, n):
        for side in range(2):
            arrived(
                nb.at[stage, h, n, side],
                rss.at[stage, h, n, 2 + side],
                rsr.at[stage, h, n, 2 + side],
            )
        return (
            on_chip(stage, h, n, 0) + nb[stage, h, n, 0].astype(F32) + nb[stage, h, n, 1].astype(F32)
        )

    def columns(p):
        return pl.ds(pl.multiple_of(p * bw, bw), bw)

    def cr_start(i):
        for k in range(1, 8):
            p = (t + k) % 8
            remote(
                dpart.at[i, :, columns(p)], drs.at[i, k], crs.at[i, k], crr.at[i, k], (g, p)
            )

    def cr_total(i):
        total = dpart[i, :, columns(t)].astype(F32)
        for k in range(1, 8):
            arrived(drs.at[i, k], crs.at[i, k], crr.at[i, k])
            total = total + drs[i, k].astype(F32)
        return total

    def dp_start(i, block):
        dpb[i, g] = block
        for k in range(1, groups):
            remote(
                dpb.at[i, g], dpb.at[i, g], dps.at[i, k], dpr_sem.at[i, k], ((g + k) % groups, t)
            )

    def dp_total(i):
        for k in range(1, groups):
            source = (g + groups - k) % groups
            arrived(dpb.at[i, source], dps.at[i, k], dpr_sem.at[i, k])
        return dpb[i].reshape(nreq, bw)

    def ca_start(i, block):
        dag[i, :, columns(t)] = block
        for k in range(1, 8):
            mine = dag.at[i, :, columns(t)]
            remote(mine, mine, cas.at[i, k], car.at[i, k], (g, (t + k) % 8))

    def ca_finish(i):
        for k in range(1, 8):
            arrived(dag.at[i, :, columns((t + 8 - k) % 8)], cas.at[i, k], car.at[i, k])

    def rotated(part, cosine, sine):
        return part * cosine + pltpu.roll(part, HD // 2, 1) * sine

    def project(h):
        mixed[...] = jnp.dot(xg1[h], w_qkv[...], preferred_element_type=F32)

        def one(b, carry):
            owner = 2 * ((x + b // 2) % 4) + (c + b % 2) % 2
            first = pl.multiple_of(owner * (2 * HALF) + HALF * h, HALF)
            place = pl.ds(first, HALF)
            here = pl.ds(pl.multiple_of(HALF * b, HALF), HALF)
            cosine = cos_ref[place, :]
            sine = sin_ref[place, :]
            for head in range(2):
                qb[h, head, here, :] = rotated(
                    mixed[here, HD * head : HD * (head + 1)], cosine, sine
                ).astype(BF16)
            key = rotated(mixed[here, 2 * HD : 3 * HD], cosine, sine).astype(BF16)
            value = mixed[here, 3 * HD : 4 * HD].astype(BF16)
            cached = pl.ds(pl.multiple_of(stored + first, HALF), HALF)
            kall[cached, :] = key
            vall[cached, :] = value
            pent_ref[0, place, :] = key
            pent_ref[1, place, :] = value
            return carry

        lax.fori_loop(0, 8, one, 0)

    def attend(h, i):
        rows = 4 * HALF
        here = pl.ds(rows * i, rows)
        query = jnp.concatenate([qb[h, 0, here, :], qb[h, 1, here, :]], axis=0)
        scores = lax.dot_general(query, kall[...], NT, preferred_element_type=F32)
        r = lax.broadcasted_iota(jnp.int32, (2 * rows, 1), 0)
        b = 4 * i + ((r >> 5) & 3)
        owner = 2 * ((x + (b >> 1)) & 3) + ((c + (b & 1)) & 1)
        q_place = owner * (2 * HALF) + HALF * h + (r & 31)
        col = lax.broadcasted_iota(jnp.int32, (1, stored + fresh), 1)
        k_place = jnp.where(
            col < stored, jnp.where(col < off_ref[0], -1, stored + fresh), col - stored
        )
        scores = jnp.where(k_place <= q_place, scores, NEGATIVE)
        top = jnp.max(scores, axis=-1, keepdims=True)
        weights = jnp.exp2((scores - top) * scale2)
        total = jnp.sum(weights, axis=-1, keepdims=True)
        result = jnp.dot(weights.astype(BF16), vall[...], preferred_element_type=F32)
        result = (result / total).astype(BF16)
        att[h, here, 0:HD] = result[:rows]
        att[h, here, HD : 2 * HD] = result[rows:]

    def out_project(h):
        for n in range(CHUNKS):
            part = jnp.dot(
                att[h], w_out[:, cw * n : cw * (n + 1)], preferred_element_type=F32
            )
            rs_split(0, h, n, part)

    def middle(h):
        mine = pl.ds(HALF * h, HALF)
        pieces = []
        for n in range(CHUNKS):
            cols = slice(cw * n, cw * (n + 1))
            value = (rows_ref[mine, cols].astype(F32) + rs_total(0, h, n)).astype(BF16)
            resid[mine, cols] = value
            pieces.append(value.astype(F32))
        values = jnp.concatenate(pieces, axis=1)
        xg2[h, 0:HALF, :] = normed(values, fgain_ref[...])
        ag_start(1, h)

    def gated(h):
        count = 8 * HALF + (slots if h == 0 else 0)
        step = 256

        def one(j, carry):
            cols = pl.ds(pl.multiple_of(j * step, step), step)
            inner = xg2[h, 0:count, :]
            gate_part = jnp.dot(inner, w_gate[:, cols], preferred_element_type=F32)
            up_part = jnp.dot(inner, w_up[:, cols], preferred_element_type=F32)
            hid[h, 0:count, cols] = (
                gate_part / (1.0 + jnp.exp(-gate_part)) * up_part
            ).astype(BF16)
            return carry

        lax.fori_loop(0, units // step, one, 0)

    def lower(h):
        count = 8 * HALF + (slots if h == 0 else 0)
        for n in range(CHUNKS):
            cols = slice(cw * n, cw * (n + 1))
            part = jnp.dot(hid[h, 0:count, :], w_down[:, cols], preferred_element_type=F32)
            rs_split(1, h, n, part)
            if h == 0:
                dpart[2, :, cols] = part[8 * HALF :].astype(BF16)

    def last(h):
        mine = pl.ds(HALF * h, HALF)
        for n in range(CHUNKS):
            cols = slice(cw * n, cw * (n + 1))
            pout_ref[mine, cols] = (resid[mine, cols].astype(F32) + rs_total(1, h, n)).astype(BF16)

    wide = 16 * slots

    def marker(head, flip):
        shape = (slots, wide) if flip else (wide, slots)
        row = lax.broadcasted_iota(jnp.int32, shape, 1 if flip else 0)
        slot = lax.broadcasted_iota(jnp.int32, shape, 0 if flip else 1)
        return (row == 16 * slot + head).astype(F32).astype(BF16)

    def decode_project():
        inner = normed(dag[0].astype(F32), again_ref[...])
        part = jnp.dot(inner, w_qkv[...], preferred_element_type=F32)
        cosine = cos_ref[fresh : fresh + slots, :]
        sine = sin_ref[fresh : fresh + slots, :]
        spread = jnp.zeros((wide, HD), F32)
        for head in range(2):
            query = rotated(part[:, HD * head : HD * (head + 1)], cosine, sine).astype(BF16)
            spread = spread + jnp.dot(marker(head, False), query, preferred_element_type=F32)
        qpad[...] = spread.astype(BF16)
        key = rotated(part[:, 2 * HD : 3 * HD], cosine, sine).astype(BF16)
        value = part[:, 3 * HD : 4 * HD].astype(BF16)
        dent_ref[0] = key
        dent_ref[1] = value
        knew[...] = jnp.zeros_like(knew)
        vnew[...] = jnp.zeros_like(vnew)
        knew[0:slots, :] = key
        vnew[0:slots, :] = value

    def decode_attend():
        def score(n, carry):
            here = pl.ds(pl.multiple_of(16 * n, 16), 16)
            part = lax.dot_general(qpad[here, :], kdec[n], NT, preferred_element_type=F32)
            col = lax.broadcasted_iota(jnp.int32, (16, dstored), 1)
            dsc[here, 0:dstored] = jnp.where(col < len_ref[n], part, NEGATIVE)
            return carry

        lax.fori_loop(0, slots, score, 0, unroll=4)
        own = lax.dot_general(qpad[...], knew[...], NT, preferred_element_type=F32)
        row = lax.broadcasted_iota(jnp.int32, (wide, HD), 0)
        col = lax.broadcasted_iota(jnp.int32, (wide, HD), 1)
        dsc[:, dstored:] = jnp.where(col == (row >> 4), own, NEGATIVE)
        scores = dsc[...]
        top = jnp.max(scores, axis=-1, keepdims=True)
        weights = jnp.exp2((scores - top) * scale2)
        total = jnp.sum(weights, axis=-1, keepdims=True)
        dpr[...] = weights.astype(BF16)

        def mix(n, carry):
            here = pl.ds(pl.multiple_of(16 * n, 16), 16)
            dob[here, :] = jnp.dot(dpr[here, 0:dstored], vdec[n], preferred_element_type=F32)
            return carry

        lax.fori_loop(0, slots, mix, 0, unroll=4)
        result = dob[...] + jnp.dot(dpr[:, dstored:], vnew[...], preferred_element_type=F32)
        result = (result / total).astype(BF16)
        picked = [
            jnp.dot(marker(head, True), result, preferred_element_type=F32).astype(BF16)
            for head in range(2)
        ]
        attended = jnp.concatenate(picked, axis=1)
        dpart[1] = jnp.dot(attended, w_out[...], preferred_element_type=F32).astype(BF16)

    for h in range(2):
        mine = pl.ds(HALF * h, HALF)
        xg1[h, 0:HALF, :] = normed(rows_ref[mine, :].astype(F32), again_ref[...])
    pair = drows_ref[...].astype(F32)
    spot = lax.broadcasted_iota(jnp.int32, (slots, width), 0)
    dpart[0] = (
        jnp.where(spot == 2 * t, pair[0:1], 0.0) + jnp.where(spot == 2 * t + 1, pair[1:2], 0.0)
    ).astype(BF16)

    pl.semaphore_wait(barrier, 6 + groups)

    ag_start(0, 0)
    cr_start(0)
    ag_start(0, 1)
    ag_forward(0, 0)
    dp_start(0, cr_total(0).astype(BF16))
    ag_forward(0, 1)
    request = lax.broadcasted_iota(jnp.int32, (nreq, nreq), 0)
    holder = (request == deal_ref[...]).astype(F32).astype(BF16)
    member = lax.broadcasted_iota(jnp.int32, (slots, nreq), 0) + slots * g
    listed = lax.broadcasted_iota(jnp.int32, (slots, nreq), 1)
    picker = lax.dot_general(
        (member == listed).astype(F32).astype(BF16), holder, NT, preferred_element_type=F32
    ).astype(BF16)
    ag_far(0, 0)
    ag_finish(0, 0)
    local["qkv"].wait()
    project(0)
    ag_far(0, 1)
    chooser = (member == deal_ref[...]).astype(F32).astype(BF16)
    ca_start(0, jnp.dot(chooser, dp_total(0), preferred_element_type=F32).astype(BF16))
    ag_finish(0, 1)
    project(1)
    local["pk"].wait()
    local["pv"].wait()
    local["out"].wait()
    attend(0, 0)
    attend(0, 1)
    out_project(0)
    attend(1, 0)
    for n in range(CHUNKS):
        rs_combine(0, 0, n)
    attend(1, 1)
    for n in range(CHUNKS):
        rs_relay(0, 0, n)
    out_project(1)
    ca_finish(0)
    decode_project()
    for n in range(CHUNKS):
        rs_combine(0, 1, n)
    middle(0)
    for n in range(CHUNKS):
        rs_relay(0, 1, n)
    local["dk"].wait()
    local["dv"].wait()
    decode_attend()
    cr_start(1)
    ag_forward(1, 0)
    middle(1)
    total = dag[0, :, columns(t)].astype(F32) + cr_total(1)
    ca_start(1, total.astype(BF16))
    ag_far(1, 0)
    ag_forward(1, 1)
    ca_finish(1)
    xg2[0, 8 * HALF :, :] = normed(dag[1].astype(F32), fgain_ref[...])
    local["gate"].wait()
    local["up"].wait()
    local["down"].wait()
    ag_finish(1, 0)
    gated(0)
    ag_far(1, 1)
    lower(0)
    cr_start(2)
    for n in range(CHUNKS):
        rs_combine(1, 0, n)
    ag_finish(1, 1)
    gated(1)
    for n in range(CHUNKS):
        rs_relay(1, 0, n)
    total = dag[1, :, columns(t)].astype(F32) + cr_total(2)
    dp_start(1, total.astype(BF16))
    lower(1)
    for n in range(CHUNKS):
        rs_combine(1, 1, n)
    ca_start(2, jnp.dot(picker, dp_total(1), preferred_element_type=F32).astype(BF16))
    for n in range(CHUNKS):
        rs_relay(1, 1, n)
    last(0)
    last(1)
    ca_finish(2)
    every = dag[2].astype(F32)
    first = jnp.sum(jnp.where(spot == 2 * t, every, 0.0), axis=0, keepdims=True)
    second = jnp.sum(jnp.where(spot == 2 * t + 1, every, 0.0), axis=0, keepdims=True)
    dout_ref[...] = jnp.concatenate([first, second], axis=0).astype(BF16)

    for copy in sends:
        copy.wait_send()


def rotary_tables(places):
    lane = jnp.arange(HD, dtype=jnp.int32)
    powers = (lane % (HD // 2)).astype(F32) * (2.0 / HD)
    angles = places.astype(F32)[:, None] * (THETA ** (-powers))[None, :]
    sign = jnp.where(lane < HD // 2, -1.0, 1.0).astype(F32)
    return jnp.cos(angles), jnp.sin(angles) * sign[None, :]


def on_device(
    groups,
    prefill_rows,
    decode_rows,
    deal_order,
    prefill_offset,
    cache_length,
    prefill_cache,
    decode_cache,
    qkv_weight,
    out_weight,
    attention_gain,
    forward_gain,
    gate_weight,
    up_weight,
    down_weight,
):
    width = prefill_rows.shape[1]
    fresh = 8 * prefill_rows.shape[0]
    slots = cache_length.shape[0]
    stored = prefill_cache.shape[2]
    dstored = decode_cache.shape[2]
    units = gate_weight.shape[1]
    places = jnp.concatenate(
        [prefill_offset[0] + jnp.arange(fresh, dtype=jnp.int32), cache_length]
    )
    cosine, sine = rotary_tables(places)
    cw = width // CHUNKS
    bw = width // 8
    vmem = pl.BlockSpec(memory_space=pltpu.VMEM)
    smem = pl.BlockSpec(memory_space=pltpu.SMEM)
    hbm = pl.BlockSpec(memory_space=pl.ANY)
    dma = pltpu.SemaphoreType.DMA
    shape = jax.ShapeDtypeStruct
    return pl.pallas_call(
        functools.partial(layer_kernel, groups),
        name="layer",
        out_shape=(
            shape(prefill_rows.shape, BF16),
            shape(decode_rows.shape, BF16),
            shape((2, fresh, HD), BF16),
            shape((2, slots, HD), BF16),
        ),
        in_specs=[vmem, vmem, vmem, smem, smem, vmem, vmem, vmem, vmem] + [hbm] * 7,
        out_specs=(vmem, vmem, vmem, vmem),
        scratch_shapes=[
            pltpu.VMEM((width, 4 * HD), BF16),
            pltpu.VMEM((2 * HD, width), BF16),
            pltpu.VMEM((width, units), BF16),
            pltpu.VMEM((width, units), BF16),
            pltpu.VMEM((units, width), BF16),
            pltpu.VMEM((stored + fresh, HD), BF16),
            pltpu.VMEM((stored + fresh, HD), BF16),
            pltpu.VMEM((slots, dstored, HD), BF16),
            pltpu.VMEM((slots, dstored, HD), BF16),
            pltpu.VMEM((2, 8 * HALF, width), BF16),
            pltpu.VMEM((2, 8 * HALF + slots, width), BF16),
            pltpu.VMEM((8 * HALF, 4 * HD), F32),
            pltpu.VMEM((2, 2, 8 * HALF, HD), BF16),
            pltpu.VMEM((2, 8 * HALF, 2 * HD), BF16),
            pltpu.VMEM((2, 2, CHUNKS, 2, 4, HALF, cw), BF16),
            pltpu.VMEM((2, 2, CHUNKS, 4, HALF, cw), BF16),
            pltpu.VMEM((2, 2, CHUNKS, 4, HALF, cw), BF16),
            pltpu.VMEM((2, 2, CHUNKS, HALF, cw), BF16),
            pltpu.VMEM((2, 2, CHUNKS, 2, HALF, cw), BF16),
            pltpu.VMEM(prefill_rows.shape, BF16),
            pltpu.VMEM((2, 8 * HALF + slots, units), BF16),
            pltpu.VMEM((3, slots, width), BF16),
            pltpu.VMEM((3, 8, slots, bw), BF16),
            pltpu.VMEM((2, groups, slots, bw), BF16),
            pltpu.VMEM((3, slots, width), BF16),
            pltpu.VMEM((16 * slots, dstored + HD), F32),
            pltpu.VMEM((16 * slots, dstored + HD), BF16),
            pltpu.VMEM((16 * slots, HD), BF16),
            pltpu.VMEM((HD, HD), BF16),
            pltpu.VMEM((HD, HD), BF16),
            pltpu.VMEM((16 * slots, HD), F32),
            dma((9,)),
            dma((2, 2, 14)),
            dma((2, 2, 14)),
            dma((2, 2, CHUNKS, 4)),
            dma((2, 2, CHUNKS, 4)),
            dma((3, 8)),
            dma((3, 8)),
            dma((2, groups)),
            dma((2, groups)),
            dma((3, 8)),
            dma((3, 8)),
        ],
        compiler_params=pltpu.CompilerParams(
            collective_id=0, has_side_effects=True, vmem_limit_bytes=66_000_000
        ),
    )(
        prefill_rows,
        decode_rows,
        deal_order[None, :],
        prefill_offset,
        cache_length,
        cosine,
        sine,
        attention_gain[None, :],
        forward_gain[None, :],
        prefill_cache,
        decode_cache,
        qkv_weight.reshape(width, 4 * HD),
        out_weight,
        gate_weight,
        up_weight,
        down_weight,
    )


def solution(mesh):
    placed = (
        P(("dp", "tensor"), None),
        P(("dp", "tensor"), None),
        P(),
        P("dp"),
        P("dp"),
        P(None, "dp", None, "tensor"),
        P(None, "dp", None, "tensor"),
        P(None, "tensor", None),
        P("tensor", None),
        P(),
        P(),
        P(None, "tensor"),
        P(None, "tensor"),
        P("tensor", None),
    )
    return jax.shard_map(
        functools.partial(on_device, mesh.shape["dp"]),
        mesh=mesh,
        in_specs=placed,
        out_specs=(
            P(("dp", "tensor"), None),
            P(("dp", "tensor"), None),
            P(None, "dp", "tensor"),
            P(None, "dp", "tensor"),
        ),
        check_vma=False,
    )
```

time: 378 us -> 87.5 us (0.23)
  waiting for transfers between devices: 261 us -> 0 us
  Pallas kernels: 0 us -> 77.4 us
  matrix products: 45.3 us -> 0 us
  other arithmetic: 22.3 us -> 2.52 us
  between operations: 15.8 us -> 1.3 us
  blocking collectives: 14 us -> 0 us
  local copies, waits for them, and re-layouts: 16.6 us -> 5.93 us
    all_gather x3 -> x0, waiting for transfers between devices: 109 us -> none  [the longest x1 61.6 us: on_device(): everyone = lax.all_gather(decode_rows, ('dp', 'tensor'), axis=0, tiled=True)]
    pallas_call x0 -> x1, Pallas kernels: none -> 77.4 us  [on_device(): pl.pallas_call(functools.partial(layer_kernel, groups), name='layer', out...]
    psum x1 -> x0, waiting for transfers between devices: 66.7 us -> none  [on_device(): fill_sum, step_sum = lax.psum((fill_part, step_part), 'tensor')]
    unnamed x7 -> x0, waiting for transfers between devices: 56.7 us -> none
    dot_general x17 -> x0, matrix products: 45.3 us -> none  [the longest x2 15.5 us: feed_forward(): return jnp.dot(hidden, down_weight, preferred_element_type=jnp.float32)]
    reduce_scatter x1 -> x0, waiting for transfers between devices: 28.1 us -> none  [on_device(): lax.psum_scatter(fill_more.astype(jnp.bfloat16), 'tensor', scatter_dimens...]
    all_gather x1 -> x0, blocking collectives: 14 us -> none  [on_device(): lax.all_gather(dealt, 'tensor', axis=0, tiled=True)]
    reduce_sum x6 -> x0, other arithmetic: 9.36 us -> none  [the longest x4 7.37 us: root_norm(): spread = jnp.mean(values * values, axis=-1, keepdims=True)]
  transfers between devices with their start and end apart: 6 -> 0, of which waited for: 5 -> 0; matrix products, arithmetic and copies ran while one was open for 15% -> 0% of each run, Pallas kernels for 0% -> 0%
where the time goes in v1:
time: 87.5 us; the launch traced here: 87.2 us
  Pallas kernels  77.4 us (88%)
  local copies, waits for them, and re-layouts  5.93 us (7%)
  other arithmetic  2.52 us (3%)
  between operations  1.3 us (1%)
    pallas_call x1, Pallas kernels, on_device(): pl.pallas_call(functools.partial(layer_kernel, groups), name='layer', out...  77.4 us
    unnamed x4, local copies, waits for them, and re-layouts  5.93 us
    mul x1, other arithmetic, rotary_tables(): return (jnp.cos(angles), jnp.sin(angles) * sign[None, :])  1.84 us

profile of v1, /device:TPU:1, one launch (start us, length us, event | category | flops | bytes accessed | tf_op | source)
XLA Modules:
  0.0 87.2 jit_solution(11727147529176149398)
XLA Ops:
  1.3 0.7 add_convert_fusion
  2.0 1.8 %fusion = (f32[528,128]{1,0:T(8,128)}, f32[528,128]{1,0:T(8,128)}) fusion(f32[128]{0:T(128)S(1)} %get-tuple-element.6, f32[128]{0:T(128)S(1)} %get-tuple-element.7, f32[528]{0:T(1024)S(1)} %add_convert_fusion), kind=kLoop, calls=%fused_computation.2 | loop fusion | flops 135168 | bytes 543808 | tf_op jit(solution)/shard_map/mul | solution.py:565
  3.8 77.4 %layer.1 = (bf16[64,2048]{1,0:T(8,128)(2,1)}, bf16[2,2048]{1,0:T(2,128)(2,1)}, bf16[2,512,128]{2,1,0:T(8,128)(2,1)}, bf16[2,16,128]{2,1,0:T(8,128)(2,1)}) custom-call(bf16[64,2048]{1,0:T(8,128)(2,1)} %rows_ref.1, bf16[2,2048]{1,0:T(2,128)(2,1)} %drows_ref.1, s32[1,256]{1,0:T(1,128)} %bitcast.9, s32[1]{0:T(128)} %copy.22.off_ref, s32[16]{0:T(128)} %len_ref.1, ...), custom_call_target="tpu_custom_call" | custom-call | tf_op jit(solution)/shard_map/layer/pallas_call | solution.py:602
  81.2 1.7 %copy.23 = bf16[64,2048]{1,0:T(8,128)(2,1)} copy(bf16[64,2048]{1,0:T(8,128)(2,1)} %get-tuple-element.12) | data formatting | bytes 524288
  82.9 1.3 %copy.24 = bf16[2,2048]{1,0:T(2,128)(2,1)} copy(bf16[2,2048]{1,0:T(2,128)(2,1)} %get-tuple-element.13) | data formatting | bytes 16384
  84.2 1.7 %copy.25 = bf16[2,512,128]{2,1,0:T(8,128)(2,1)} copy(bf16[2,512,128]{2,1,0:T(8,128)(2,1)} %get-tuple-element.14) | data formatting | bytes 524288
  85.9 1.3 %copy.26 = bf16[2,16,128]{2,1,0:T(8,128)(2,1)} copy(bf16[2,16,128]{2,1,0:T(8,128)(2,1)} %get-tuple-element.15) | data formatting | bytes 16384
  (2 shorter events, 0.0 us)

commit v2 on v1

--- a/solution.py
+++ b/solution.py
@@ -16,8 +16,10 @@
 F32 = jnp.float32
 BF16 = jnp.bfloat16
 NT = (((1,), (1,)), ((), ()))
-HALF = 32
-CHUNKS = 4
+BATCHES = 4
+SIZE = 16
+JOINED = 1
+CHUNKS = 2
 
 
 def normed(values, gain):
@@ -32,8 +34,6 @@
     deal_ref,
     off_ref,
     len_ref,
-    cos_ref,
-    sin_ref,
     again_ref,
     fgain_ref,
     pcache,
@@ -58,7 +58,8 @@
     vdec,
     xg1,
     xg2,
-    mixed,
+    kplace,
+    dtotal,
     qb,
     att,
     pb,
@@ -78,6 +79,8 @@
     knew,
     vnew,
     dob,
+    cos_ref,
+    sin_ref,
     wsem,
     ags,
     agr,
@@ -149,7 +152,10 @@
         return (xg1 if stage == 0 else xg2).at[h]
 
     def ag_block(stage, h, b, p):
-        return buffer_of(stage, h).at[pl.ds(HALF * b + 16 * p, 16)]
+        rows = pl.ds(SIZE * b, SIZE)
+        if p is None:
+            return buffer_of(stage, h).at[rows]
+        return buffer_of(stage, h).at[rows, pl.ds(width // 2 * p, width // 2)]
 
     def ag_send(stage, h, src_b, dst_b, p, number, dev):
         remote(
@@ -164,47 +170,36 @@
         arrived(ag_block(stage, h, b, p), ags.at[stage, h, number], agr.at[stage, h, number])
 
     def ag_start(stage, h):
-        ag_send(stage, h, 0, 6, 0, 1, right)
+        ag_send(stage, h, 0, 4, 0, 1, right)
         ag_send(stage, h, 0, 2, 1, 4, left)
-        ag_send(stage, h, 0, 6, 1, 2, right)
+        ag_send(stage, h, 0, 4, 1, 2, right)
         ag_send(stage, h, 0, 2, 0, 3, left)
-        ag_send(stage, h, 0, 1, 0, 0, partner)
-        ag_send(stage, h, 0, 1, 1, 13, partner)
-
-    def ag_forward(stage, h):
-        ag_wait(stage, h, 6, 0, 1)
-        ag_send(stage, h, 6, 4, 0, 5, right)
+        ag_send(stage, h, 0, 1, None, 0, partner)
+
+    def ag_onward(stage, h):
+        ag_wait(stage, h, 4, 0, 1)
+        ag_send(stage, h, 4, 6, 0, 5, right)
         ag_wait(stage, h, 2, 1, 4)
-        ag_send(stage, h, 2, 4, 1, 6, left)
-        ag_send(stage, h, 6, 7, 0, 7, partner)
-        ag_send(stage, h, 2, 3, 1, 10, partner)
-        ag_wait(stage, h, 6, 1, 2)
-        ag_send(stage, h, 6, 7, 1, 8, partner)
+        ag_send(stage, h, 2, 6, 1, 6, left)
+
+    def ag_share(stage, h):
+        ag_wait(stage, h, 4, 1, 2)
+        ag_send(stage, h, 4, 5, None, 7, partner)
         ag_wait(stage, h, 2, 0, 3)
-        ag_send(stage, h, 2, 3, 0, 9, partner)
+        ag_send(stage, h, 2, 3, None, 8, partner)
 
     def ag_far(stage, h):
-        ag_wait(stage, h, 4, 0, 5)
-        ag_send(stage, h, 4, 5, 0, 11, partner)
-        ag_wait(stage, h, 4, 1, 6)
-        ag_send(stage, h, 4, 5, 1, 12, partner)
+        ag_wait(stage, h, 6, 0, 5)
+        ag_wait(stage, h, 6, 1, 6)
+        ag_send(stage, h, 6, 7, None, 9, partner)
 
     def ag_finish(stage, h):
-        for b, p, number in (
-            (1, 0, 0),
-            (1, 1, 13),
-            (7, 0, 7),
-            (3, 1, 10),
-            (7, 1, 8),
-            (3, 0, 9),
-            (5, 0, 11),
-            (5, 1, 12),
-        ):
-            ag_wait(stage, h, b, p, number)
+        for b, number in ((1, 0), (5, 7), (3, 8), (7, 9)):
+            ag_wait(stage, h, b, None, number)
 
     def rs_split(stage, h, n, part):
         for b in range(8):
-            pb[stage, h, n, b % 2, b // 2] = part[HALF * b : HALF * (b + 1)].astype(BF16)
+            pb[stage, h, n, b % 2, b // 2] = part[SIZE * b : SIZE * (b + 1)].astype(BF16)
         remote(
             pb.at[stage, h, n, 1],
             rcv.at[stage, h, n],
@@ -226,23 +221,31 @@
             dev,
         )
 
-    def rs_combine(stage, h, n):
+    def rs_combine(stage, h):
+        for n in range(CHUNKS):
+            rs_combine_chunk(stage, h, n)
+
+    def rs_relay(stage, h):
+        for n in range(CHUNKS):
+            rs_relay_chunk(stage, h, n)
+
+    def rs_combine_chunk(stage, h, n):
         arrived(rcv.at[stage, h, n], rss.at[stage, h, n, 0], rsr.at[stage, h, n, 0])
-        cb[stage, h, n, 2] = on_chip(stage, h, n, 2).astype(BF16)
+        cb[stage, h, n, 3] = on_chip(stage, h, n, 3).astype(BF16)
         remote(
-            cb.at[stage, h, n, 2],
+            cb.at[stage, h, n, 3],
             fb.at[stage, h, n],
             rss.at[stage, h, n, 1],
             rsr.at[stage, h, n, 1],
             right if n % 2 == 0 else left,
         )
-        d = 3 if n % 2 == 0 else 1
+        d = 2 if n % 2 == 0 else 1
         cb[stage, h, n, d] = on_chip(stage, h, n, d).astype(BF16)
         to_side(stage, h, n, d)
 
-    def rs_relay(stage, h, n):
+    def rs_relay_chunk(stage, h, n):
         arrived(fb.at[stage, h, n], rss.at[stage, h, n, 1], rsr.at[stage, h, n, 1])
-        d = 1 if n % 2 == 0 else 3
+        d = 1 if n % 2 == 0 else 2
         cb[stage, h, n, d] = (on_chip(stage, h, n, d) + fb[stage, h, n].astype(F32)).astype(BF16)
         to_side(stage, h, n, d)
 
@@ -300,62 +303,58 @@
     def rotated(part, cosine, sine):
         return part * cosine + pltpu.roll(part, HD // 2, 1) * sine
 
+    def owner_of(b):
+        d = b // 2
+        return 2 * ((x + d + (d // 2) * (5 - 2 * d)) % 4) + (c + b % 2) % 2
+
+    part_rows = 8 * SIZE
+
+    def place_of(index):
+        b = (index // SIZE) % 8
+        d = b >> 1
+        owner = 2 * ((x + (d ^ (d >> 1))) & 3) + ((c + (b & 1)) & 1)
+        return owner * (BATCHES * SIZE) + SIZE * (index // part_rows) + index % SIZE
+
     def project(h):
-        mixed[...] = jnp.dot(xg1[h], w_qkv[...], preferred_element_type=F32)
-
-        def one(b, carry):
-            owner = 2 * ((x + b // 2) % 4) + (c + b % 2) % 2
-            first = pl.multiple_of(owner * (2 * HALF) + HALF * h, HALF)
-            place = pl.ds(first, HALF)
-            here = pl.ds(pl.multiple_of(HALF * b, HALF), HALF)
-            cosine = cos_ref[place, :]
-            sine = sin_ref[place, :]
-            for head in range(2):
-                qb[h, head, here, :] = rotated(
-                    mixed[here, HD * head : HD * (head + 1)], cosine, sine
-                ).astype(BF16)
-            key = rotated(mixed[here, 2 * HD : 3 * HD], cosine, sine).astype(BF16)
-            value = mixed[here, 3 * HD : 4 * HD].astype(BF16)
-            cached = pl.ds(pl.multiple_of(stored + first, HALF), HALF)
-            kall[cached, :] = key
-            vall[cached, :] = value
-            pent_ref[0, place, :] = key
-            pent_ref[1, place, :] = value
-            return carry
-
-        lax.fori_loop(0, 8, one, 0)
-
-    def attend(h, i):
-        rows = 4 * HALF
-        here = pl.ds(rows * i, rows)
-        query = jnp.concatenate([qb[h, 0, here, :], qb[h, 1, here, :]], axis=0)
+        part = jnp.dot(xg1[h], w_qkv[...], preferred_element_type=F32)
+        here = slice(part_rows * h, part_rows * (h + 1))
+        there = slice(stored + part_rows * h, stored + part_rows * (h + 1))
+        cosine = cos_ref[here, :]
+        sine = sin_ref[here, :]
+        for head in range(2):
+            qb[h, head] = rotated(part[:, HD * head : HD * (head + 1)], cosine, sine).astype(BF16)
+        kall[there, :] = rotated(part[:, 2 * HD : 3 * HD], cosine, sine).astype(BF16)
+        vall[there, :] = part[:, 3 * HD : 4 * HD].astype(BF16)
+
+    def entries(h):
+        for b in range(8):
+            first = pl.multiple_of(owner_of(b) * (BATCHES * SIZE) + SIZE * h, SIZE)
+            here = pl.ds(stored + part_rows * h + SIZE * b, SIZE)
+            pent_ref[0, pl.ds(first, SIZE), :] = kall[here, :]
+            pent_ref[1, pl.ds(first, SIZE), :] = vall[here, :]
+
+    def attend(h):
+        rows = part_rows
+        query = qb[h].reshape(2 * rows, HD)
         scores = lax.dot_general(query, kall[...], NT, preferred_element_type=F32)
         r = lax.broadcasted_iota(jnp.int32, (2 * rows, 1), 0)
-        b = 4 * i + ((r >> 5) & 3)
-        owner = 2 * ((x + (b >> 1)) & 3) + ((c + (b & 1)) & 1)
-        q_place = owner * (2 * HALF) + HALF * h + (r & 31)
-        col = lax.broadcasted_iota(jnp.int32, (1, stored + fresh), 1)
-        k_place = jnp.where(
-            col < stored, jnp.where(col < off_ref[0], -1, stored + fresh), col - stored
-        )
+        q_place = place_of(rows * h + r % rows)
+        k_place = kplace[...]
         scores = jnp.where(k_place <= q_place, scores, NEGATIVE)
         top = jnp.max(scores, axis=-1, keepdims=True)
         weights = jnp.exp2((scores - top) * scale2)
         total = jnp.sum(weights, axis=-1, keepdims=True)
         result = jnp.dot(weights.astype(BF16), vall[...], preferred_element_type=F32)
         result = (result / total).astype(BF16)
-        att[h, here, 0:HD] = result[:rows]
-        att[h, here, HD : 2 * HD] = result[rows:]
-
-    def out_project(h):
-        for n in range(CHUNKS):
-            part = jnp.dot(
-                att[h], w_out[:, cw * n : cw * (n + 1)], preferred_element_type=F32
-            )
-            rs_split(0, h, n, part)
+        att[h, :, 0:HD] = result[:rows]
+        att[h, :, HD : 2 * HD] = result[rows:]
+
+    def out_project(h, n):
+        part = jnp.dot(att[h], w_out[:, cw * n : cw * (n + 1)], preferred_element_type=F32)
+        rs_split(0, h, n, part)
 
     def middle(h):
-        mine = pl.ds(HALF * h, HALF)
+        mine = pl.ds(SIZE * h, SIZE)
         pieces = []
         for n in range(CHUNKS):
             cols = slice(cw * n, cw * (n + 1))
@@ -363,11 +362,13 @@
             resid[mine, cols] = value
             pieces.append(value.astype(F32))
         values = jnp.concatenate(pieces, axis=1)
-        xg2[h, 0:HALF, :] = normed(values, fgain_ref[...])
+        xg2[h, 0:SIZE, :] = normed(values, fgain_ref[...])
         ag_start(1, h)
 
-    def gated(h):
-        count = 8 * HALF + (slots if h == 0 else 0)
+    steps = units // 256
+
+    def gated(h, begin=0, end=steps):
+        count = 8 * SIZE + (slots if h == JOINED else 0)
         step = 256
 
         def one(j, carry):
@@ -375,24 +376,23 @@
             inner = xg2[h, 0:count, :]
             gate_part = jnp.dot(inner, w_gate[:, cols], preferred_element_type=F32)
             up_part = jnp.dot(inner, w_up[:, cols], preferred_element_type=F32)
-            hid[h, 0:count, cols] = (
+            hid[0:count, cols] = (
                 gate_part / (1.0 + jnp.exp(-gate_part)) * up_part
             ).astype(BF16)
             return carry
 
-        lax.fori_loop(0, units // step, one, 0)
-
-    def lower(h):
-        count = 8 * HALF + (slots if h == 0 else 0)
-        for n in range(CHUNKS):
-            cols = slice(cw * n, cw * (n + 1))
-            part = jnp.dot(hid[h, 0:count, :], w_down[:, cols], preferred_element_type=F32)
-            rs_split(1, h, n, part)
-            if h == 0:
-                dpart[2, :, cols] = part[8 * HALF :].astype(BF16)
+        lax.fori_loop(begin, end, one, 0)
+
+    def lower(h, n):
+        count = 8 * SIZE + (slots if h == JOINED else 0)
+        cols = slice(cw * n, cw * (n + 1))
+        part = jnp.dot(hid[0:count, :], w_down[:, cols], preferred_element_type=F32)
+        rs_split(1, h, n, part)
+        if h == JOINED:
+            dpart[2, :, cols] = part[8 * SIZE :].astype(BF16)
 
     def last(h):
-        mine = pl.ds(HALF * h, HALF)
+        mine = pl.ds(SIZE * h, SIZE)
         for n in range(CHUNKS):
             cols = slice(cw * n, cw * (n + 1))
             pout_ref[mine, cols] = (resid[mine, cols].astype(F32) + rs_total(1, h, n)).astype(BF16)
@@ -424,7 +424,7 @@
         knew[0:slots, :] = key
         vnew[0:slots, :] = value
 
-    def decode_attend():
+    def decode_attend(begin, end):
         def score(n, carry):
             here = pl.ds(pl.multiple_of(16 * n, 16), 16)
             part = lax.dot_general(qpad[here, :], kdec[n], NT, preferred_element_type=F32)
@@ -432,7 +432,9 @@
             dsc[here, 0:dstored] = jnp.where(col < len_ref[n], part, NEGATIVE)
             return carry
 
-        lax.fori_loop(0, slots, score, 0, unroll=4)
+        lax.fori_loop(begin, end, score, 0, unroll=4)
+
+    def decode_weigh():
         own = lax.dot_general(qpad[...], knew[...], NT, preferred_element_type=F32)
         row = lax.broadcasted_iota(jnp.int32, (wide, HD), 0)
         col = lax.broadcasted_iota(jnp.int32, (wide, HD), 1)
@@ -440,9 +442,10 @@
         scores = dsc[...]
         top = jnp.max(scores, axis=-1, keepdims=True)
         weights = jnp.exp2((scores - top) * scale2)
-        total = jnp.sum(weights, axis=-1, keepdims=True)
+        dtotal[...] = jnp.sum(weights, axis=-1, keepdims=True)
         dpr[...] = weights.astype(BF16)
 
+    def decode_mix():
         def mix(n, carry):
             here = pl.ds(pl.multiple_of(16 * n, 16), 16)
             dob[here, :] = jnp.dot(dpr[here, 0:dstored], vdec[n], preferred_element_type=F32)
@@ -450,7 +453,7 @@
 
         lax.fori_loop(0, slots, mix, 0, unroll=4)
         result = dob[...] + jnp.dot(dpr[:, dstored:], vnew[...], preferred_element_type=F32)
-        result = (result / total).astype(BF16)
+        result = (result / dtotal[...]).astype(BF16)
         picked = [
             jnp.dot(marker(head, True), result, preferred_element_type=F32).astype(BF16)
             for head in range(2)
@@ -458,23 +461,43 @@
         attended = jnp.concatenate(picked, axis=1)
         dpart[1] = jnp.dot(attended, w_out[...], preferred_element_type=F32).astype(BF16)
 
-    for h in range(2):
-        mine = pl.ds(HALF * h, HALF)
-        xg1[h, 0:HALF, :] = normed(rows_ref[mine, :].astype(F32), again_ref[...])
+    for h in range(BATCHES):
+        mine = pl.ds(SIZE * h, SIZE)
+        xg1[h, 0:SIZE, :] = normed(rows_ref[mine, :].astype(F32), again_ref[...])
     pair = drows_ref[...].astype(F32)
     spot = lax.broadcasted_iota(jnp.int32, (slots, width), 0)
     dpart[0] = (
         jnp.where(spot == 2 * t, pair[0:1], 0.0) + jnp.where(spot == 2 * t + 1, pair[1:2], 0.0)
     ).astype(BF16)
 
-    pl.semaphore_wait(barrier, 6 + groups)
-
-    ag_start(0, 0)
-    cr_start(0)
-    ag_start(0, 1)
-    ag_forward(0, 0)
-    dp_start(0, cr_total(0).astype(BF16))
-    ag_forward(0, 1)
+    lane = lax.broadcasted_iota(jnp.int32, (1, HD), 1)
+    powers = (lane % (HD // 2)).astype(F32) * (2.0 / HD)
+    inverse = jnp.exp(powers * (-math.log(THETA)))
+    sign = jnp.where(lane < HD // 2, -1.0, 1.0).astype(F32)
+
+    def table(first, count, places):
+        angles = places.astype(F32) * inverse
+        cos_ref[pl.ds(first, count), :] = jnp.cos(angles)
+        sin_ref[pl.ds(first, count), :] = jnp.sin(angles) * sign
+
+    def some(i, carry):
+        row = lax.broadcasted_iota(jnp.int32, (64, HD), 0)
+        table(pl.multiple_of(64 * i, 64), 64, off_ref[0] + place_of(64 * i + row))
+        return carry
+
+    lax.fori_loop(0, fresh // 64, some, 0)
+    col = lax.broadcasted_iota(jnp.int32, (1, stored + fresh), 1)
+    kplace[...] = jnp.where(
+        col < stored,
+        jnp.where(col < off_ref[0], -1, fresh),
+        place_of(jnp.maximum(col - stored, 0)),
+    )
+    slot = lax.broadcasted_iota(jnp.int32, (slots, HD), 0)
+    length = jnp.zeros((slots, HD), jnp.int32)
+    for n in range(slots):
+        length = jnp.where(slot == n, len_ref[n], length)
+    table(fresh, slots, length)
+
     request = lax.broadcasted_iota(jnp.int32, (nreq, nreq), 0)
     holder = (request == deal_ref[...]).astype(F32).astype(BF16)
     member = lax.broadcasted_iota(jnp.int32, (slots, nreq), 0) + slots * g
@@ -482,87 +505,172 @@
     picker = lax.dot_general(
         (member == listed).astype(F32).astype(BF16), holder, NT, preferred_element_type=F32
     ).astype(BF16)
+    chooser = (member == deal_ref[...]).astype(F32).astype(BF16)
+
+    def dealt():
+        ca_start(0, jnp.dot(chooser, dp_total(0), preferred_element_type=F32).astype(BF16))
+
+    def decode_middle():
+        total = dag[0, :, columns(t)].astype(F32) + cr_total(1)
+        ca_start(1, total.astype(BF16))
+
+    def decode_inner():
+        ca_finish(1)
+        xg2[JOINED, part_rows:, :] = normed(dag[1].astype(F32), fgain_ref[...])
+
+    def decode_last():
+        total = dag[1, :, columns(t)].astype(F32) + cr_total(2)
+        dp_start(1, total.astype(BF16))
+
+    def undealt():
+        ca_start(2, jnp.dot(picker, dp_total(1), preferred_element_type=F32).astype(BF16))
+
+    def decode_out():
+        ca_finish(2)
+        every = dag[2].astype(F32)
+        first = jnp.sum(jnp.where(spot == 2 * t, every, 0.0), axis=0, keepdims=True)
+        second = jnp.sum(jnp.where(spot == 2 * t + 1, every, 0.0), axis=0, keepdims=True)
+        dout_ref[...] = jnp.concatenate([first, second], axis=0).astype(BF16)
+
+    pl.semaphore_wait(barrier, 6 + groups)
+
+    ag_start(0, 0)
+    ag_start(0, 1)
+    cr_start(0)
+    ag_start(0, 2)
+    ag_start(0, 3)
+    ag_onward(0, 0)
+    ag_share(0, 0)
+    ag_onward(0, 1)
+    ag_share(0, 1)
+    ag_onward(0, 2)
+    dp_start(0, cr_total(0).astype(BF16))
+    ag_share(0, 2)
+    ag_onward(0, 3)
+    ag_share(0, 3)
     ag_far(0, 0)
+    ag_far(0, 1)
+    local["qkv"].wait()
     ag_finish(0, 0)
-    local["qkv"].wait()
     project(0)
-    ag_far(0, 1)
-    chooser = (member == deal_ref[...]).astype(F32).astype(BF16)
-    ca_start(0, jnp.dot(chooser, dp_total(0), preferred_element_type=F32).astype(BF16))
+    ag_far(0, 2)
+    dealt()
     ag_finish(0, 1)
     project(1)
+    ag_far(0, 3)
+    entries(1)
+    entries(0)
+    ag_finish(0, 2)
+    project(2)
+    entries(2)
+    ag_finish(0, 3)
+    project(3)
     local["pk"].wait()
     local["pv"].wait()
     local["out"].wait()
-    attend(0, 0)
-    attend(0, 1)
-    out_project(0)
-    attend(1, 0)
-    for n in range(CHUNKS):
-        rs_combine(0, 0, n)
-    attend(1, 1)
-    for n in range(CHUNKS):
-        rs_relay(0, 0, n)
-    out_project(1)
+    attend(0)
+    out_project(0, 0)
+    out_project(0, 1)
+    attend(1)
+    out_project(1, 0)
+    entries(3)
+    out_project(1, 1)
+    rs_combine(0, 0)
     ca_finish(0)
     decode_project()
-    for n in range(CHUNKS):
-        rs_combine(0, 1, n)
+    local["dk"].wait()
+    decode_attend(0, slots // 2)
+    rs_combine(0, 1)
+    attend(2)
+    out_project(2, 0)
+    out_project(2, 1)
+    attend(3)
+    rs_relay(0, 0)
+    out_project(3, 0)
+    out_project(3, 1)
+    rs_combine(0, 2)
+    decode_attend(slots // 2, slots)
+    decode_weigh()
+    rs_relay(0, 1)
+    rs_combine(0, 3)
+    local["dv"].wait()
+    decode_mix()
     middle(0)
-    for n in range(CHUNKS):
-        rs_relay(0, 1, n)
-    local["dk"].wait()
-    local["dv"].wait()
-    decode_attend()
     cr_start(1)
-    ag_forward(1, 0)
+    rs_relay(0, 2)
     middle(1)
-    total = dag[0, :, columns(t)].astype(F32) + cr_total(1)
-    ca_start(1, total.astype(BF16))
+    rs_relay(0, 3)
+    ag_onward(1, 0)
+    ag_share(1, 0)
+    middle(2)
+    decode_middle()
+    ag_onward(1, 1)
+    ag_share(1, 1)
+    middle(3)
     ag_far(1, 0)
-    ag_forward(1, 1)
-    ca_finish(1)
-    xg2[0, 8 * HALF :, :] = normed(dag[1].astype(F32), fgain_ref[...])
+    ag_onward(1, 2)
     local["gate"].wait()
     local["up"].wait()
     local["down"].wait()
     ag_finish(1, 0)
-    gated(0)
+    gated(0, 0, steps // 2)
+    ag_share(1, 2)
+    gated(0, steps // 2, steps)
     ag_far(1, 1)
-    lower(0)
+    lower(0, 0)
+    decode_inner()
+    lower(0, 1)
+    ag_onward(1, 3)
+    ag_finish(1, 1)
+    gated(1, 0, steps // 2)
+    gated(1, steps // 2, steps)
+    ag_far(1, 2)
+    rs_combine(1, 0)
+    lower(1, 0)
+    lower(1, 1)
     cr_start(2)
-    for n in range(CHUNKS):
-        rs_combine(1, 0, n)
-    ag_finish(1, 1)
-    gated(1)
-    for n in range(CHUNKS):
-        rs_relay(1, 0, n)
-    total = dag[1, :, columns(t)].astype(F32) + cr_total(2)
-    dp_start(1, total.astype(BF16))
-    lower(1)
-    for n in range(CHUNKS):
-        rs_combine(1, 1, n)
-    ca_start(2, jnp.dot(picker, dp_total(1), preferred_element_type=F32).astype(BF16))
-    for n in range(CHUNKS):
-        rs_relay(1, 1, n)
+    ag_share(1, 3)
+    ag_finish(1, 2)
+    gated(2, 0, steps // 2)
+    ag_far(1, 3)
+    gated(2, steps // 2, steps)
+    rs_combine(1, 1)
+    lower(2, 0)
+    lower(2, 1)
+    ag_finish(1, 3)
+    gated(3, 0, steps // 2)
+    rs_relay(1, 0)
+    gated(3, steps // 2, steps)
+    rs_combine(1, 2)
+    lower(3, 0)
+    decode_last()
+    lower(3, 1)
+    rs_relay(1, 1)
     last(0)
+    rs_combine(1, 3)
+    rs_relay(1, 2)
     last(1)
-    ca_finish(2)
-    every = dag[2].astype(F32)
-    first = jnp.sum(jnp.where(spot == 2 * t, every, 0.0), axis=0, keepdims=True)
-    second = jnp.sum(jnp.where(spot == 2 * t + 1, every, 0.0), axis=0, keepdims=True)
-    dout_ref[...] = jnp.concatenate([first, second], axis=0).astype(BF16)
+    undealt()
+    rs_relay(1, 3)
+    last(2)
+    decode_out()
+    last(3)
 
     for copy in sends:
         copy.wait_send()
 
 
-def rotary_tables(places):
-    lane = jnp.arange(HD, dtype=jnp.int32)
-    powers = (lane % (HD // 2)).astype(F32) * (2.0 / HD)
-    angles = places.astype(F32)[:, None] * (THETA ** (-powers))[None, :]
-    sign = jnp.where(lane < HD // 2, -1.0, 1.0).astype(F32)
-    return jnp.cos(angles), jnp.sin(angles) * sign[None, :]
+def hand_out(*refs):
+    count = len(refs) // 3 + 1
+    sources, targets, sems = refs[:count], refs[count : 2 * count], refs[2 * count]
+    copies = [
+        pltpu.make_async_copy(source, target, sems.at[i])
+        for i, (source, target) in enumerate(zip(sources, targets))
+    ]
+    for copy in copies:
+        copy.start()
+    for copy in copies:
+        copy.wait()
 
 
 def on_device(
@@ -588,10 +696,6 @@
     stored = prefill_cache.shape[2]
     dstored = decode_cache.shape[2]
     units = gate_weight.shape[1]
-    places = jnp.concatenate(
-        [prefill_offset[0] + jnp.arange(fresh, dtype=jnp.int32), cache_length]
-    )
-    cosine, sine = rotary_tables(places)
     cw = width // CHUNKS
     bw = width // 8
     vmem = pl.BlockSpec(memory_space=pltpu.VMEM)
@@ -599,7 +703,7 @@
     hbm = pl.BlockSpec(memory_space=pl.ANY)
     dma = pltpu.SemaphoreType.DMA
     shape = jax.ShapeDtypeStruct
-    return pl.pallas_call(
+    results = pl.pallas_call(
         functools.partial(layer_kernel, groups),
         name="layer",
         out_shape=(
@@ -608,7 +712,7 @@
             shape((2, fresh, HD), BF16),
             shape((2, slots, HD), BF16),
         ),
-        in_specs=[vmem, vmem, vmem, smem, smem, vmem, vmem, vmem, vmem] + [hbm] * 7,
+        in_specs=[vmem, vmem, vmem, smem, smem, vmem, vmem] + [hbm] * 7,
         out_specs=(vmem, vmem, vmem, vmem),
         scratch_shapes=[
             pltpu.VMEM((width, 4 * HD), BF16),
@@ -620,18 +724,19 @@
             pltpu.VMEM((stored + fresh, HD), BF16),
             pltpu.VMEM((slots, dstored, HD), BF16),
             pltpu.VMEM((slots, dstored, HD), BF16),
-            pltpu.VMEM((2, 8 * HALF, width), BF16),
-            pltpu.VMEM((2, 8 * HALF + slots, width), BF16),
-            pltpu.VMEM((8 * HALF, 4 * HD), F32),
-            pltpu.VMEM((2, 2, 8 * HALF, HD), BF16),
-            pltpu.VMEM((2, 8 * HALF, 2 * HD), BF16),
-            pltpu.VMEM((2, 2, CHUNKS, 2, 4, HALF, cw), BF16),
-            pltpu.VMEM((2, 2, CHUNKS, 4, HALF, cw), BF16),
-            pltpu.VMEM((2, 2, CHUNKS, 4, HALF, cw), BF16),
-            pltpu.VMEM((2, 2, CHUNKS, HALF, cw), BF16),
-            pltpu.VMEM((2, 2, CHUNKS, 2, HALF, cw), BF16),
+            pltpu.VMEM((BATCHES, 8 * SIZE, width), BF16),
+            pltpu.VMEM((BATCHES, 8 * SIZE + slots, width), BF16),
+            pltpu.VMEM((1, stored + fresh), jnp.int32),
+            pltpu.VMEM((16 * slots, 1), F32),
+            pltpu.VMEM((BATCHES, 2, 8 * SIZE, HD), BF16),
+            pltpu.VMEM((BATCHES, 8 * SIZE, 2 * HD), BF16),
+            pltpu.VMEM((2, BATCHES, CHUNKS, 2, 4, SIZE, cw), BF16),
+            pltpu.VMEM((2, BATCHES, CHUNKS, 4, SIZE, cw), BF16),
+            pltpu.VMEM((2, BATCHES, CHUNKS, 4, SIZE, cw), BF16),
+            pltpu.VMEM((2, BATCHES, CHUNKS, SIZE, cw), BF16),
+            pltpu.VMEM((2, BATCHES, CHUNKS, 2, SIZE, cw), BF16),
             pltpu.VMEM(prefill_rows.shape, BF16),
-            pltpu.VMEM((2, 8 * HALF + slots, units), BF16),
+            pltpu.VMEM((8 * SIZE + slots, units), BF16),
             pltpu.VMEM((3, slots, width), BF16),
             pltpu.VMEM((3, 8, slots, bw), BF16),
             pltpu.VMEM((2, groups, slots, bw), BF16),
@@ -642,11 +747,13 @@
             pltpu.VMEM((HD, HD), BF16),
             pltpu.VMEM((HD, HD), BF16),
             pltpu.VMEM((16 * slots, HD), F32),
+            pltpu.VMEM((fresh + slots, HD), F32),
+            pltpu.VMEM((fresh + slots, HD), F32),
             dma((9,)),
-            dma((2, 2, 14)),
-            dma((2, 2, 14)),
-            dma((2, 2, CHUNKS, 4)),
-            dma((2, 2, CHUNKS, 4)),
+            dma((2, BATCHES, 10)),
+            dma((2, BATCHES, 10)),
+            dma((2, BATCHES, CHUNKS, 4)),
+            dma((2, BATCHES, CHUNKS, 4)),
             dma((3, 8)),
             dma((3, 8)),
             dma((2, groups)),
@@ -663,8 +770,6 @@
         deal_order[None, :],
         prefill_offset,
         cache_length,
-        cosine,
-        sine,
         attention_gain[None, :],
         forward_gain[None, :],
         prefill_cache,
@@ -675,6 +780,14 @@
         up_weight,
         down_weight,
     )
+    return pl.pallas_call(
+        hand_out,
+        name="hand_out",
+        out_shape=tuple(shape(result.shape, BF16) for result in results),
+        in_specs=[vmem] * 4,
+        out_specs=(hbm,) * 4,
+        scratch_shapes=[dma((4,))],
+    )(*results)
 
 
 def solution(mesh):

time: 87.5 us -> 75.2 us (0.86)
  local copies, waits for them, and re-layouts: 5.93 us -> 0 us
  Pallas kernels: 77.4 us -> 73.6 us
  other arithmetic: 2.52 us -> 0 us
    unnamed x4 -> x0, local copies, waits for them, and re-layouts: 5.93 us -> none
    pallas_call x1, Pallas kernels: 77.4 us -> 71.7 us  [on_device(): pl.pallas_call(functools.partial(layer_kernel, groups), name='layer', out...]
    pallas_call x0 -> x1, Pallas kernels: none -> 1.88 us  [on_device(): pl.pallas_call(hand_out, name='hand_out', out_shape=tuple((shape(result.s...]
    mul x1 -> x0, other arithmetic: 1.84 us -> none  [rotary_tables(): return (jnp.cos(angles), jnp.sin(angles) * sign[None, :])]
where the time goes in v2:
time: 75.2 us; the launch traced here: 75 us
  Pallas kernels  73.6 us (98%)
  between operations  1.45 us (2%)
    pallas_call x1, Pallas kernels, on_device(): pl.pallas_call(functools.partial(layer_kernel, groups), name='layer', out...  71.7 us
    pallas_call x1, Pallas kernels, on_device(): pl.pallas_call(hand_out, name='hand_out', out_shape=tuple((shape(result.s...  1.88 us

profile of v2, /device:TPU:1, one launch (start us, length us, event | category | flops | bytes accessed | tf_op | source)
XLA Modules:
  0.0 75.0 jit_solution(2874219247516823464)
XLA Ops:
  1.3 71.7 %layer.1 = (bf16[64,2048]{1,0:T(8,128)(2,1)}, bf16[2,2048]{1,0:T(2,128)(2,1)}, bf16[2,512,128]{2,1,0:T(8,128)(2,1)}, bf16[2,16,128]{2,1,0:T(8,128)(2,1)}) custom-call(bf16[64,2048]{1,0:T(8,128)(2,1)} %rows_ref.1, bf16[2,2048]{1,0:T(2,128)(2,1)} %drows_ref.1, s32[1,256]{1,0:T(1,128)} %bitcast.7, s32[1]{0:T(128)S(6)} %copy.18.off_ref, s32[16]{0:T(128)} %len_ref.1, ...), custom_call_target="tpu_custom_call" | custom-call | tf_op jit(solution)/shard_map/layer/pallas_call | solution.py:706
  73.0 1.9 %hand_out.1 = (bf16[64,2048]{1,0:T(8,128)(2,1)}, bf16[2,2048]{1,0:T(2,128)(2,1)}, bf16[2,512,128]{2,1,0:T(8,128)(2,1)}, bf16[2,16,128]{2,1,0:T(8,128)(2,1)}) custom-call(bf16[64,2048]{1,0:T(8,128)(2,1)} %get-tuple-element.8.refs_0_, bf16[2,2048]{1,0:T(2,128)(2,1)} %get-tuple-element.9.refs_1_, bf16[2,512,128]{2,1,0:T(8,128)(2,1)} %get-tuple-element.10.refs_2_, ...), custom_call_target="tpu_custom_call" | custom-call | tf_op jit(solution)/shard_map/hand_out/pallas_call | solution.py:783

commit v3 on v2

--- a/solution.py
+++ b/solution.py
@@ -18,7 +18,7 @@
 NT = (((1,), (1,)), ((), ()))
 BATCHES = 4
 SIZE = 16
-JOINED = 1
+JOINED = 0
 CHUNKS = 2
 
 
@@ -59,6 +59,8 @@
     xg1,
     xg2,
     kplace,
+    picker,
+    chooser,
     dtotal,
     qb,
     att,
@@ -92,6 +94,7 @@
     dpr_sem,
     cas,
     car,
+    passed,
 ):
     g = lax.axis_index("dp")
     t = lax.axis_index("tensor")
@@ -142,11 +145,15 @@
     fetch("up", 7, up_hbm, w_up)
     fetch("down", 8, down_hbm, w_down)
 
+    deep = min(4, groups)
+    high = groups // deep
+    below = [(g // deep) * deep + (g + k) % deep for k in range(1, deep)]
+    across = [(g + deep * k) % groups for k in range(1, high)]
     barrier = pltpu.get_barrier_semaphore()
     for k in range(1, 8):
         pl.semaphore_signal(barrier, inc=1, device_id=(g, (t + k) % 8), device_id_type=MESH)
-    for k in range(1, groups):
-        pl.semaphore_signal(barrier, inc=1, device_id=((g + k) % groups, t), device_id_type=MESH)
+    for other in below + across:
+        pl.semaphore_signal(barrier, inc=1, device_id=(other, t), device_id_type=MESH)
 
     def buffer_of(stage, h):
         return (xg1 if stage == 0 else xg2).at[h]
@@ -223,25 +230,23 @@
 
     def rs_combine(stage, h):
         for n in range(CHUNKS):
-            rs_combine_chunk(stage, h, n)
+            arrived(rcv.at[stage, h, n], rss.at[stage, h, n, 0], rsr.at[stage, h, n, 0])
+            cb[stage, h, n, 3] = on_chip(stage, h, n, 3).astype(BF16)
+            remote(
+                cb.at[stage, h, n, 3],
+                fb.at[stage, h, n],
+                rss.at[stage, h, n, 1],
+                rsr.at[stage, h, n, 1],
+                right if n % 2 == 0 else left,
+            )
+        for n in range(CHUNKS):
+            d = 2 if n % 2 == 0 else 1
+            cb[stage, h, n, d] = on_chip(stage, h, n, d).astype(BF16)
+            to_side(stage, h, n, d)
 
     def rs_relay(stage, h):
         for n in range(CHUNKS):
             rs_relay_chunk(stage, h, n)
-
-    def rs_combine_chunk(stage, h, n):
-        arrived(rcv.at[stage, h, n], rss.at[stage, h, n, 0], rsr.at[stage, h, n, 0])
-        cb[stage, h, n, 3] = on_chip(stage, h, n, 3).astype(BF16)
-        remote(
-            cb.at[stage, h, n, 3],
-            fb.at[stage, h, n],
-            rss.at[stage, h, n, 1],
-            rsr.at[stage, h, n, 1],
-            right if n % 2 == 0 else left,
-        )
-        d = 2 if n % 2 == 0 else 1
-        cb[stage, h, n, d] = on_chip(stage, h, n, d).astype(BF16)
-        to_side(stage, h, n, d)
 
     def rs_relay_chunk(stage, h, n):
         arrived(fb.at[stage, h, n], rss.at[stage, h, n, 1], rsr.at[stage, h, n, 1])
@@ -461,54 +466,65 @@
         attended = jnp.concatenate(picked, axis=1)
         dpart[1] = jnp.dot(attended, w_out[...], preferred_element_type=F32).astype(BF16)
 
-    for h in range(BATCHES):
+    def own_rows(h):
         mine = pl.ds(SIZE * h, SIZE)
         xg1[h, 0:SIZE, :] = normed(rows_ref[mine, :].astype(F32), again_ref[...])
-    pair = drows_ref[...].astype(F32)
+
     spot = lax.broadcasted_iota(jnp.int32, (slots, width), 0)
-    dpart[0] = (
-        jnp.where(spot == 2 * t, pair[0:1], 0.0) + jnp.where(spot == 2 * t + 1, pair[1:2], 0.0)
-    ).astype(BF16)
-
-    lane = lax.broadcasted_iota(jnp.int32, (1, HD), 1)
-    powers = (lane % (HD // 2)).astype(F32) * (2.0 / HD)
-    inverse = jnp.exp(powers * (-math.log(THETA)))
-    sign = jnp.where(lane < HD // 2, -1.0, 1.0).astype(F32)
-
-    def table(first, count, places):
-        angles = places.astype(F32) * inverse
-        cos_ref[pl.ds(first, count), :] = jnp.cos(angles)
-        sin_ref[pl.ds(first, count), :] = jnp.sin(angles) * sign
-
-    def some(i, carry):
-        row = lax.broadcasted_iota(jnp.int32, (64, HD), 0)
-        table(pl.multiple_of(64 * i, 64), 64, off_ref[0] + place_of(64 * i + row))
-        return carry
-
-    lax.fori_loop(0, fresh // 64, some, 0)
-    col = lax.broadcasted_iota(jnp.int32, (1, stored + fresh), 1)
-    kplace[...] = jnp.where(
-        col < stored,
-        jnp.where(col < off_ref[0], -1, fresh),
-        place_of(jnp.maximum(col - stored, 0)),
-    )
-    slot = lax.broadcasted_iota(jnp.int32, (slots, HD), 0)
-    length = jnp.zeros((slots, HD), jnp.int32)
-    for n in range(slots):
-        length = jnp.where(slot == n, len_ref[n], length)
-    table(fresh, slots, length)
-
-    request = lax.broadcasted_iota(jnp.int32, (nreq, nreq), 0)
-    holder = (request == deal_ref[...]).astype(F32).astype(BF16)
+
+    def own_decode_rows():
+        pair = drows_ref[...].astype(F32)
+        dpart[0] = (
+            jnp.where(spot == 2 * t, pair[0:1], 0.0) + jnp.where(spot == 2 * t + 1, pair[1:2], 0.0)
+        ).astype(BF16)
+
+    def tables():
+        lane = lax.broadcasted_iota(jnp.int32, (1, HD), 1)
+        powers = (lane % (HD // 2)).astype(F32) * (2.0 / HD)
+        inverse = jnp.exp(powers * (-math.log(THETA)))
+        sign = jnp.where(lane < HD // 2, -1.0, 1.0).astype(F32)
+
+        def table(first, count, places):
+            angles = places.astype(F32) * inverse
+            cos_ref[pl.ds(first, count), :] = jnp.cos(angles)
+            sin_ref[pl.ds(first, count), :] = jnp.sin(angles) * sign
+
+        def some(i, carry):
+            row = lax.broadcasted_iota(jnp.int32, (64, HD), 0)
+            table(pl.multiple_of(64 * i, 64), 64, off_ref[0] + place_of(64 * i + row))
+            return carry
+
+        lax.fori_loop(0, fresh // 64, some, 0)
+        col = lax.broadcasted_iota(jnp.int32, (1, stored + fresh), 1)
+        kplace[...] = jnp.where(
+            col < stored,
+            jnp.where(col < off_ref[0], -1, fresh),
+            place_of(jnp.maximum(col - stored, 0)),
+        )
+        slot = lax.broadcasted_iota(jnp.int32, (slots, HD), 0)
+        length = jnp.zeros((slots, HD), jnp.int32)
+        for n in range(slots):
+            length = jnp.where(slot == n, len_ref[n], length)
+        table(fresh, slots, length)
+
     member = lax.broadcasted_iota(jnp.int32, (slots, nreq), 0) + slots * g
     listed = lax.broadcasted_iota(jnp.int32, (slots, nreq), 1)
-    picker = lax.dot_general(
-        (member == listed).astype(F32).astype(BF16), holder, NT, preferred_element_type=F32
-    ).astype(BF16)
-    chooser = (member == deal_ref[...]).astype(F32).astype(BF16)
+
+    def choices():
+        request = lax.broadcasted_iota(jnp.int32, (nreq, nreq), 0)
+        holder = (request == deal_ref[...]).astype(F32).astype(BF16)
+        picker[...] = lax.dot_general(
+            (member == listed).astype(F32).astype(BF16), holder, NT, preferred_element_type=F32
+        ).astype(BF16)
+        chooser[...] = (member == deal_ref[...]).astype(F32).astype(BF16)
+
+    def first_deal():
+        if across:
+            pl.semaphore_wait(passed, len(across))
+        dp_start(0, cr_total(0).astype(BF16))
 
     def dealt():
-        ca_start(0, jnp.dot(chooser, dp_total(0), preferred_element_type=F32).astype(BF16))
+        ca_start(0, jnp.dot(chooser[...], dp_total(0), preferred_element_type=F32).astype(BF16))
 
     def decode_middle():
         total = dag[0, :, columns(t)].astype(F32) + cr_total(1)
@@ -523,7 +539,7 @@
         dp_start(1, total.astype(BF16))
 
     def undealt():
-        ca_start(2, jnp.dot(picker, dp_total(1), preferred_element_type=F32).astype(BF16))
+        ca_start(2, jnp.dot(picker[...], dp_total(1), preferred_element_type=F32).astype(BF16))
 
     def decode_out():
         ca_finish(2)
@@ -532,34 +548,44 @@
         second = jnp.sum(jnp.where(spot == 2 * t + 1, every, 0.0), axis=0, keepdims=True)
         dout_ref[...] = jnp.concatenate([first, second], axis=0).astype(BF16)
 
-    pl.semaphore_wait(barrier, 6 + groups)
+    own_decode_rows()
+    own_rows(0)
+    own_rows(1)
+
+    pl.semaphore_wait(barrier, 7 + len(below) + len(across))
+    for other in across:
+        pl.semaphore_signal(passed, inc=1, device_id=(other, t), device_id_type=MESH)
+
 
     ag_start(0, 0)
     ag_start(0, 1)
+    own_rows(2)
+    ag_start(0, 2)
+    own_rows(3)
+    ag_start(0, 3)
+    tables()
+    choices()
     cr_start(0)
-    ag_start(0, 2)
-    ag_start(0, 3)
     ag_onward(0, 0)
     ag_share(0, 0)
     ag_onward(0, 1)
     ag_share(0, 1)
     ag_onward(0, 2)
-    dp_start(0, cr_total(0).astype(BF16))
     ag_share(0, 2)
     ag_onward(0, 3)
     ag_share(0, 3)
     ag_far(0, 0)
+    first_deal()
     ag_far(0, 1)
     local["qkv"].wait()
     ag_finish(0, 0)
     project(0)
     ag_far(0, 2)
-    dealt()
+    entries(0)
     ag_finish(0, 1)
     project(1)
     ag_far(0, 3)
     entries(1)
-    entries(0)
     ag_finish(0, 2)
     project(2)
     entries(2)
@@ -569,46 +595,48 @@
     local["pv"].wait()
     local["out"].wait()
     attend(0)
+    entries(3)
     out_project(0, 0)
     out_project(0, 1)
     attend(1)
+    dealt()
     out_project(1, 0)
-    entries(3)
     out_project(1, 1)
     rs_combine(0, 0)
+    attend(2)
+    out_project(2, 0)
+    out_project(2, 1)
+    rs_combine(0, 1)
+    attend(3)
+    out_project(3, 0)
+    out_project(3, 1)
+    rs_combine(0, 2)
+    rs_relay(0, 0)
     ca_finish(0)
     decode_project()
     local["dk"].wait()
     decode_attend(0, slots // 2)
-    rs_combine(0, 1)
-    attend(2)
-    out_project(2, 0)
-    out_project(2, 1)
-    attend(3)
-    rs_relay(0, 0)
-    out_project(3, 0)
-    out_project(3, 1)
-    rs_combine(0, 2)
+    rs_relay(0, 1)
+    rs_combine(0, 3)
     decode_attend(slots // 2, slots)
     decode_weigh()
-    rs_relay(0, 1)
-    rs_combine(0, 3)
     local["dv"].wait()
     decode_mix()
+    cr_start(1)
     middle(0)
-    cr_start(1)
     rs_relay(0, 2)
     middle(1)
     rs_relay(0, 3)
     ag_onward(1, 0)
+    decode_middle()
     ag_share(1, 0)
     middle(2)
-    decode_middle()
     ag_onward(1, 1)
     ag_share(1, 1)
     middle(3)
     ag_far(1, 0)
     ag_onward(1, 2)
+    decode_inner()
     local["gate"].wait()
     local["up"].wait()
     local["down"].wait()
@@ -618,43 +646,42 @@
     gated(0, steps // 2, steps)
     ag_far(1, 1)
     lower(0, 0)
-    decode_inner()
+    ag_onward(1, 3)
     lower(0, 1)
-    ag_onward(1, 3)
+    cr_start(2)
+    ag_share(1, 3)
     ag_finish(1, 1)
     gated(1, 0, steps // 2)
+    ag_far(1, 2)
     gated(1, steps // 2, steps)
-    ag_far(1, 2)
     rs_combine(1, 0)
     lower(1, 0)
     lower(1, 1)
-    cr_start(2)
-    ag_share(1, 3)
+    ag_far(1, 3)
     ag_finish(1, 2)
     gated(2, 0, steps // 2)
-    ag_far(1, 3)
     gated(2, steps // 2, steps)
     rs_combine(1, 1)
+    decode_last()
     lower(2, 0)
+    rs_relay(1, 0)
     lower(2, 1)
     ag_finish(1, 3)
     gated(3, 0, steps // 2)
-    rs_relay(1, 0)
     gated(3, steps // 2, steps)
     rs_combine(1, 2)
     lower(3, 0)
-    decode_last()
     lower(3, 1)
     rs_relay(1, 1)
     last(0)
     rs_combine(1, 3)
     rs_relay(1, 2)
+    undealt()
     last(1)
-    undealt()
     rs_relay(1, 3)
     last(2)
+    last(3)
     decode_out()
-    last(3)
 
     for copy in sends:
         copy.wait_send()
@@ -727,6 +754,8 @@
             pltpu.VMEM((BATCHES, 8 * SIZE, width), BF16),
             pltpu.VMEM((BATCHES, 8 * SIZE + slots, width), BF16),
             pltpu.VMEM((1, stored + fresh), jnp.int32),
+            pltpu.VMEM((slots, groups * slots), BF16),
+            pltpu.VMEM((slots, groups * slots), BF16),
             pltpu.VMEM((16 * slots, 1), F32),
             pltpu.VMEM((BATCHES, 2, 8 * SIZE, HD), BF16),
             pltpu.VMEM((BATCHES, 8 * SIZE, 2 * HD), BF16),
@@ -760,6 +789,7 @@
             dma((2, groups)),
             dma((3, 8)),
             dma((3, 8)),
+            pltpu.SemaphoreType.REGULAR,
         ],
         compiler_params=pltpu.CompilerParams(
             collective_id=0, has_side_effects=True, vmem_limit_bytes=66_000_000

time: 75.2 us -> 70.8 us (0.941)
  Pallas kernels: 73.6 us -> 69.2 us
    pallas_call x1, Pallas kernels: 71.7 us -> 67.3 us  [on_device(): pl.pallas_call(functools.partial(layer_kernel, groups), name='layer', out...]
where the time goes in v3:
time: 70.8 us; the launch traced here: 70.6 us
  Pallas kernels  69.2 us (98%)
  between operations  1.45 us (2%)
    pallas_call x1, Pallas kernels, on_device(): pl.pallas_call(functools.partial(layer_kernel, groups), name='layer', out...  67.3 us
    pallas_call x1, Pallas kernels, on_device(): pl.pallas_call(hand_out, name='hand_out', out_shape=tuple((shape(result.s...  1.88 us

profile of v3, /device:TPU:1, one launch (start us, length us, event | category | flops | bytes accessed | tf_op | source)
XLA Modules:
  0.0 70.6 jit_solution(2448873324090015234)
XLA Ops:
  1.3 67.3 %layer.1 = (bf16[64,2048]{1,0:T(8,128)(2,1)}, bf16[2,2048]{1,0:T(2,128)(2,1)}, bf16[2,512,128]{2,1,0:T(8,128)(2,1)}, bf16[2,16,128]{2,1,0:T(8,128)(2,1)}) custom-call(bf16[64,2048]{1,0:T(8,128)(2,1)} %rows_ref.1, bf16[2,2048]{1,0:T(2,128)(2,1)} %drows_ref.1, s32[1,256]{1,0:T(1,128)} %bitcast.7, s32[1]{0:T(128)S(6)} %copy.18.off_ref, s32[16]{0:T(128)} %len_ref.1, ...), custom_call_target="tpu_custom_call" | custom-call | tf_op jit(solution)/shard_map/layer/pallas_call | solution.py:733
  68.6 1.9 %hand_out.1 = (bf16[64,2048]{1,0:T(8,128)(2,1)}, bf16[2,2048]{1,0:T(2,128)(2,1)}, bf16[2,512,128]{2,1,0:T(8,128)(2,1)}, bf16[2,16,128]{2,1,0:T(8,128)(2,1)}) custom-call(bf16[64,2048]{1,0:T(8,128)(2,1)} %get-tuple-element.8.refs_0_, bf16[2,2048]{1,0:T(2,128)(2,1)} %get-tuple-element.9.refs_1_, bf16[2,512,128]{2,1,0:T(8,128)(2,1)} %get-tuple-element.10.refs_2_, ...), custom_call_target="tpu_custom_call" | custom-call | tf_op jit(solution)/shard_map/hand_out/pallas_call | solution.py:813

commit v4 on v3

--- a/solution.py
+++ b/solution.py
@@ -19,6 +19,8 @@
 BATCHES = 4
 SIZE = 16
 JOINED = 0
+GATHER_DIRECT = ()
+SCATTER_DIRECT = ()
 CHUNKS = 2
 
 
@@ -29,13 +31,13 @@
 
 def layer_kernel(
     groups,
-    rows_ref,
-    drows_ref,
-    deal_ref,
-    off_ref,
-    len_ref,
-    again_ref,
-    fgain_ref,
+    rows_hbm,
+    drows_hbm,
+    deal_hbm,
+    off_hbm,
+    len_hbm,
+    again_hbm,
+    fgain_hbm,
     pcache,
     dcache,
     qkv_hbm,
@@ -43,10 +45,10 @@
     gate_hbm,
     up_hbm,
     down_hbm,
-    pout_ref,
-    dout_ref,
-    pent_ref,
-    dent_ref,
+    pout_hbm,
+    dout_hbm,
+    pent_hbm,
+    dent_hbm,
     w_qkv,
     w_out,
     w_gate,
@@ -95,17 +97,29 @@
     cas,
     car,
     passed,
+    rows_ref,
+    drows_ref,
+    deal_ref,
+    off_ref,
+    len_ref,
+    again_ref,
+    fgain_ref,
+    pout_ref,
+    dout_ref,
+    pent_ref,
+    dent_ref,
+    osem,
 ):
     g = lax.axis_index("dp")
     t = lax.axis_index("tensor")
     x = t // 2
     c = t % 2
-    width = rows_ref.shape[1]
+    width = rows_hbm.shape[1]
     cw = width // CHUNKS
     bw = width // 8
     stored = pcache.shape[2]
-    fresh = pent_ref.shape[1]
-    slots = dent_ref.shape[1]
+    fresh = pent_hbm.shape[1]
+    slots = dent_hbm.shape[1]
     dstored = dcache.shape[2]
     units = w_gate.shape[1]
     nreq = groups * slots
@@ -114,6 +128,7 @@
     partner = (g, t + 1 - 2 * c)
     right = (g, ((x + 1) % 4) * 2 + c)
     left = (g, ((x + 3) % 4) * 2 + c)
+    far = (g, ((x + 2) % 4) * 2 + c)
     sends = []
 
     def remote(src, dst, ss, rs, dev):
@@ -127,23 +142,6 @@
         pltpu.make_async_remote_copy(
             src_ref=dst, dst_ref=dst, send_sem=ss, recv_sem=rs, device_id=partner, device_id_type=MESH
         ).wait_recv()
-
-    local = {}
-
-    def fetch(name, index, src, dst):
-        copy = pltpu.make_async_copy(src, dst, wsem.at[index])
-        copy.start()
-        local[name] = copy
-
-    fetch("qkv", 0, qkv_hbm, w_qkv)
-    fetch("pk", 1, pcache.at[0, 0], kall.at[pl.ds(0, stored)])
-    fetch("pv", 2, pcache.at[1, 0], vall.at[pl.ds(0, stored)])
-    fetch("out", 3, out_hbm, w_out)
-    fetch("dk", 4, dcache.at[0], kdec)
-    fetch("dv", 5, dcache.at[1], vdec)
-    fetch("gate", 6, gate_hbm, w_gate)
-    fetch("up", 7, up_hbm, w_up)
-    fetch("down", 8, down_hbm, w_down)
 
     deep = min(4, groups)
     high = groups // deep
@@ -155,6 +153,37 @@
     for other in below + across:
         pl.semaphore_signal(barrier, inc=1, device_id=(other, t), device_id_type=MESH)
 
+    local = {}
+
+    def fetch(name, src, dst):
+        copy = pltpu.make_async_copy(src, dst, wsem.at[len(local)])
+        copy.start()
+        local[name] = copy
+
+    fetch("rows", rows_hbm, rows_ref)
+    fetch("drows", drows_hbm, drows_ref)
+    fetch("again", again_hbm, again_ref)
+    fetch("off", off_hbm, off_ref)
+    fetch("len", len_hbm, len_ref)
+    fetch("deal", deal_hbm, deal_ref)
+    fetch("fgain", fgain_hbm, fgain_ref)
+    fetch("qkv", qkv_hbm, w_qkv)
+    fetch("pk", pcache.at[0, 0], kall.at[pl.ds(0, stored)])
+    fetch("pv", pcache.at[1, 0], vall.at[pl.ds(0, stored)])
+    fetch("out", out_hbm, w_out)
+    fetch("dk", dcache.at[0], kdec)
+    fetch("dv", dcache.at[1], vdec)
+    fetch("gate", gate_hbm, w_gate)
+    fetch("up", up_hbm, w_up)
+    fetch("down", down_hbm, w_down)
+
+    handed = []
+
+    def hand(source, target):
+        copy = pltpu.make_async_copy(source, target, osem.at[len(handed)])
+        copy.start()
+        handed.append(copy)
+
     def buffer_of(stage, h):
         return (xg1 if stage == 0 else xg2).at[h]
 
@@ -177,6 +206,8 @@
         arrived(ag_block(stage, h, b, p), ags.at[stage, h, number], agr.at[stage, h, number])
 
     def ag_start(stage, h):
+        if (stage, h) in GATHER_DIRECT:
+            ag_send(stage, h, 0, 6, None, 5, far)
         ag_send(stage, h, 0, 4, 0, 1, right)
         ag_send(stage, h, 0, 2, 1, 4, left)
         ag_send(stage, h, 0, 4, 1, 2, right)
@@ -184,20 +215,28 @@
         ag_send(stage, h, 0, 1, None, 0, partner)
 
     def ag_onward(stage, h):
+        if (stage, h) in GATHER_DIRECT:
+            return
         ag_wait(stage, h, 4, 0, 1)
         ag_send(stage, h, 4, 6, 0, 5, right)
         ag_wait(stage, h, 2, 1, 4)
         ag_send(stage, h, 2, 6, 1, 6, left)
 
     def ag_share(stage, h):
+        if (stage, h) in GATHER_DIRECT:
+            ag_wait(stage, h, 4, 0, 1)
+            ag_wait(stage, h, 2, 1, 4)
         ag_wait(stage, h, 4, 1, 2)
         ag_send(stage, h, 4, 5, None, 7, partner)
         ag_wait(stage, h, 2, 0, 3)
         ag_send(stage, h, 2, 3, None, 8, partner)
 
     def ag_far(stage, h):
-        ag_wait(stage, h, 6, 0, 5)
-        ag_wait(stage, h, 6, 1, 6)
+        if (stage, h) in GATHER_DIRECT:
+            ag_wait(stage, h, 6, None, 5)
+        else:
+            ag_wait(stage, h, 6, 0, 5)
+            ag_wait(stage, h, 6, 1, 6)
         ag_send(stage, h, 6, 7, None, 9, partner)
 
     def ag_finish(stage, h):
@@ -237,14 +276,17 @@
                 fb.at[stage, h, n],
                 rss.at[stage, h, n, 1],
                 rsr.at[stage, h, n, 1],
-                right if n % 2 == 0 else left,
+                far if (stage, h) in SCATTER_DIRECT else right if n % 2 == 0 else left,
             )
         for n in range(CHUNKS):
-            d = 2 if n % 2 == 0 else 1
-            cb[stage, h, n, d] = on_chip(stage, h, n, d).astype(BF16)
-            to_side(stage, h, n, d)
+            first = 2 if n % 2 == 0 else 1
+            for d in (first, 3 - first) if (stage, h) in SCATTER_DIRECT else (first,):
+                cb[stage, h, n, d] = on_chip(stage, h, n, d).astype(BF16)
+                to_side(stage, h, n, d)
 
     def rs_relay(stage, h):
+        if (stage, h) in SCATTER_DIRECT:
+            return
         for n in range(CHUNKS):
             rs_relay_chunk(stage, h, n)
 
@@ -261,9 +303,11 @@
                 rss.at[stage, h, n, 2 + side],
                 rsr.at[stage, h, n, 2 + side],
             )
-        return (
-            on_chip(stage, h, n, 0) + nb[stage, h, n, 0].astype(F32) + nb[stage, h, n, 1].astype(F32)
-        )
+        total = on_chip(stage, h, n, 0) + nb[stage, h, n, 0].astype(F32) + nb[stage, h, n, 1].astype(F32)
+        if (stage, h) in SCATTER_DIRECT:
+            arrived(fb.at[stage, h, n], rss.at[stage, h, n, 1], rsr.at[stage, h, n, 1])
+            total = total + fb[stage, h, n].astype(F32)
+        return total
 
     def columns(p):
         return pl.ds(pl.multiple_of(p * bw, bw), bw)
@@ -331,12 +375,17 @@
         kall[there, :] = rotated(part[:, 2 * HD : 3 * HD], cosine, sine).astype(BF16)
         vall[there, :] = part[:, 3 * HD : 4 * HD].astype(BF16)
 
+    entered = []
+
     def entries(h):
         for b in range(8):
             first = pl.multiple_of(owner_of(b) * (BATCHES * SIZE) + SIZE * h, SIZE)
             here = pl.ds(stored + part_rows * h + SIZE * b, SIZE)
             pent_ref[0, pl.ds(first, SIZE), :] = kall[here, :]
             pent_ref[1, pl.ds(first, SIZE), :] = vall[here, :]
+        entered.append(h)
+        if len(entered) == BATCHES:
+            hand(pent_ref, pent_hbm)
 
     def attend(h):
         rows = part_rows
@@ -401,6 +450,7 @@
         for n in range(CHUNKS):
             cols = slice(cw * n, cw * (n + 1))
             pout_ref[mine, cols] = (resid[mine, cols].astype(F32) + rs_total(1, h, n)).astype(BF16)
+        hand(pout_ref.at[mine], pout_hbm.at[mine])
 
     wide = 16 * slots
 
@@ -424,6 +474,7 @@
         value = part[:, 3 * HD : 4 * HD].astype(BF16)
         dent_ref[0] = key
         dent_ref[1] = value
+        hand(dent_ref, dent_hbm)
         knew[...] = jnp.zeros_like(knew)
         vnew[...] = jnp.zeros_like(vnew)
         knew[0:slots, :] = key
@@ -450,13 +501,14 @@
         dtotal[...] = jnp.sum(weights, axis=-1, keepdims=True)
         dpr[...] = weights.astype(BF16)
 
-    def decode_mix():
+    def decode_mix(begin, end):
         def mix(n, carry):
             here = pl.ds(pl.multiple_of(16 * n, 16), 16)
             dob[here, :] = jnp.dot(dpr[here, 0:dstored], vdec[n], preferred_element_type=F32)
             return carry
 
-        lax.fori_loop(0, slots, mix, 0, unroll=4)
+        lax.fori_loop(begin, end, mix, 0, unroll=4)
+    def decode_finish():
         result = dob[...] + jnp.dot(dpr[:, dstored:], vnew[...], preferred_element_type=F32)
         result = (result / dtotal[...]).astype(BF16)
         picked = [
@@ -547,7 +599,10 @@
         first = jnp.sum(jnp.where(spot == 2 * t, every, 0.0), axis=0, keepdims=True)
         second = jnp.sum(jnp.where(spot == 2 * t + 1, every, 0.0), axis=0, keepdims=True)
         dout_ref[...] = jnp.concatenate([first, second], axis=0).astype(BF16)
-
+        hand(dout_ref, dout_hbm)
+
+    for name in ("rows", "drows", "again", "off", "len", "deal", "fgain"):
+        local[name].wait()
     own_decode_rows()
     own_rows(0)
     own_rows(1)
@@ -557,6 +612,7 @@
         pl.semaphore_signal(passed, inc=1, device_id=(other, t), device_id_type=MESH)
 
 
+    cr_start(0)
     ag_start(0, 0)
     ag_start(0, 1)
     own_rows(2)
@@ -565,8 +621,8 @@
     ag_start(0, 3)
     tables()
     choices()
-    cr_start(0)
     ag_onward(0, 0)
+    first_deal()
     ag_share(0, 0)
     ag_onward(0, 1)
     ag_share(0, 1)
@@ -575,8 +631,8 @@
     ag_onward(0, 3)
     ag_share(0, 3)
     ag_far(0, 0)
-    first_deal()
     ag_far(0, 1)
+    dealt()
     local["qkv"].wait()
     ag_finish(0, 0)
     project(0)
@@ -595,33 +651,34 @@
     local["pv"].wait()
     local["out"].wait()
     attend(0)
-    entries(3)
     out_project(0, 0)
     out_project(0, 1)
     attend(1)
-    dealt()
     out_project(1, 0)
     out_project(1, 1)
+    entries(3)
     rs_combine(0, 0)
     attend(2)
     out_project(2, 0)
+    ca_finish(0)
+    decode_project()
+    rs_combine(0, 1)
+    local["dk"].wait()
+    decode_attend(0, slots // 2)
     out_project(2, 1)
-    rs_combine(0, 1)
     attend(3)
+    rs_relay(0, 0)
     out_project(3, 0)
     out_project(3, 1)
     rs_combine(0, 2)
-    rs_relay(0, 0)
-    ca_finish(0)
-    decode_project()
-    local["dk"].wait()
-    decode_attend(0, slots // 2)
-    rs_relay(0, 1)
-    rs_combine(0, 3)
     decode_attend(slots // 2, slots)
     decode_weigh()
+    rs_relay(0, 1)
     local["dv"].wait()
-    decode_mix()
+    decode_mix(0, slots // 2)
+    rs_combine(0, 3)
+    decode_mix(slots // 2, slots)
+    decode_finish()
     cr_start(1)
     middle(0)
     rs_relay(0, 2)
@@ -642,11 +699,11 @@
     local["down"].wait()
     ag_finish(1, 0)
     gated(0, 0, steps // 2)
-    ag_share(1, 2)
     gated(0, steps // 2, steps)
     ag_far(1, 1)
     lower(0, 0)
     ag_onward(1, 3)
+    ag_share(1, 2)
     lower(0, 1)
     cr_start(2)
     ag_share(1, 3)
@@ -657,34 +714,36 @@
     rs_combine(1, 0)
     lower(1, 0)
     lower(1, 1)
-    ag_far(1, 3)
     ag_finish(1, 2)
     gated(2, 0, steps // 2)
+    ag_far(1, 3)
     gated(2, steps // 2, steps)
+    lower(2, 0)
     rs_combine(1, 1)
     decode_last()
-    lower(2, 0)
-    rs_relay(1, 0)
     lower(2, 1)
     ag_finish(1, 3)
     gated(3, 0, steps // 2)
+    rs_relay(1, 0)
     gated(3, steps // 2, steps)
     rs_combine(1, 2)
     lower(3, 0)
     lower(3, 1)
     rs_relay(1, 1)
+    rs_combine(1, 3)
     last(0)
-    rs_combine(1, 3)
     rs_relay(1, 2)
     undealt()
     last(1)
     rs_relay(1, 3)
     last(2)
+    decode_out()
     last(3)
-    decode_out()
 
     for copy in sends:
         copy.wait_send()
+    for copy in handed:
+        copy.wait()
 
 
 def hand_out(*refs):
@@ -726,7 +785,6 @@
     cw = width // CHUNKS
     bw = width // 8
     vmem = pl.BlockSpec(memory_space=pltpu.VMEM)
-    smem = pl.BlockSpec(memory_space=pltpu.SMEM)
     hbm = pl.BlockSpec(memory_space=pl.ANY)
     dma = pltpu.SemaphoreType.DMA
     shape = jax.ShapeDtypeStruct
@@ -739,8 +797,8 @@
             shape((2, fresh, HD), BF16),
             shape((2, slots, HD), BF16),
         ),
-        in_specs=[vmem, vmem, vmem, smem, smem, vmem, vmem] + [hbm] * 7,
-        out_specs=(vmem, vmem, vmem, vmem),
+        in_specs=[pl.BlockSpec(memory_space=pltpu.HBM)] * 7 + [hbm] * 7,
+        out_specs=(hbm,) * 4,
         scratch_shapes=[
             pltpu.VMEM((width, 4 * HD), BF16),
             pltpu.VMEM((2 * HD, width), BF16),
@@ -778,7 +836,7 @@
             pltpu.VMEM((16 * slots, HD), F32),
             pltpu.VMEM((fresh + slots, HD), F32),
             pltpu.VMEM((fresh + slots, HD), F32),
-            dma((9,)),
+            dma((16,)),
             dma((2, BATCHES, 10)),
             dma((2, BATCHES, 10)),
             dma((2, BATCHES, CHUNKS, 4)),
@@ -790,6 +848,18 @@
             dma((3, 8)),
             dma((3, 8)),
             pltpu.SemaphoreType.REGULAR,
+            pltpu.VMEM(prefill_rows.shape, BF16),
+            pltpu.VMEM(decode_rows.shape, BF16),
+            pltpu.VMEM((1, groups * slots), jnp.int32),
+            pltpu.SMEM((1,), jnp.int32),
+            pltpu.SMEM((slots,), jnp.int32),
+            pltpu.VMEM((1, width), F32),
+            pltpu.VMEM((1, width), F32),
+            pltpu.VMEM(prefill_rows.shape, BF16),
+            pltpu.VMEM(decode_rows.shape, BF16),
+            pltpu.VMEM((2, fresh, HD), BF16),
+            pltpu.VMEM((2, slots, HD), BF16),
+            dma((8,)),
         ],
         compiler_params=pltpu.CompilerParams(
             collective_id=0, has_side_effects=True, vmem_limit_bytes=66_000_000

time: 70.8 us -> 69 us (0.975)
  Pallas kernels: 69.2 us -> 67.4 us
    pallas_call x1, Pallas kernels: 67.3 us -> 65.6 us  [on_device(): pl.pallas_call(functools.partial(layer_kernel, groups), name='layer', out...]
where the time goes in v4:
time: 69 us; the launch traced here: 68.9 us
  Pallas kernels  67.4 us (98%)
  between operations  1.45 us (2%)
    pallas_call x1, Pallas kernels, on_device(): pl.pallas_call(functools.partial(layer_kernel, groups), name='layer', out...  65.6 us
    pallas_call x1, Pallas kernels, on_device(): pl.pallas_call(hand_out, name='hand_out', out_shape=tuple((shape(result.s...  1.88 us

profile of v4, /device:TPU:1, one launch (start us, length us, event | category | flops | bytes accessed | tf_op | source)
XLA Modules:
  0.0 68.9 jit_solution(7428467676417257991)
XLA Ops:
  1.3 65.6 %layer.1 = (bf16[64,2048]{1,0:T(8,128)(2,1)}, bf16[2,2048]{1,0:T(2,128)(2,1)}, bf16[2,512,128]{2,1,0:T(8,128)(2,1)}, bf16[2,16,128]{2,1,0:T(8,128)(2,1)}) custom-call(bf16[64,2048]{1,0:T(8,128)(2,1)} %rows_hbm.1, bf16[2,2048]{1,0:T(2,128)(2,1)} %drows_hbm.1, s32[1,256]{1,0:T(1,128)} %bitcast.7, s32[1]{0:T(128)S(6)} %copy.18.off_hbm, s32[16]{0:T(128)} %len_hbm.1, ...), custom_call_target="tpu_custom_call" | custom-call | tf_op jit(solution)/shard_map/layer/pallas_call | solution.py:791
  66.9 1.9 %hand_out.1 = (bf16[64,2048]{1,0:T(8,128)(2,1)}, bf16[2,2048]{1,0:T(2,128)(2,1)}, bf16[2,512,128]{2,1,0:T(8,128)(2,1)}, bf16[2,16,128]{2,1,0:T(8,128)(2,1)}) custom-call(bf16[64,2048]{1,0:T(8,128)(2,1)} %get-tuple-element.8.refs_0_, bf16[2,2048]{1,0:T(2,128)(2,1)} %get-tuple-element.9.refs_1_, bf16[2,512,128]{2,1,0:T(8,128)(2,1)} %get-tuple-element.10.refs_2_, ...), custom_call_target="tpu_custom_call" | custom-call | tf_op jit(solution)/shard_map/hand_out/pallas_call | solution.py:883

commit v5 on v4

--- a/solution.py
+++ b/solution.py
@@ -419,11 +419,11 @@
         xg2[h, 0:SIZE, :] = normed(values, fgain_ref[...])
         ag_start(1, h)
 
-    steps = units // 256
+    steps = units // 512
 
     def gated(h, begin=0, end=steps):
         count = 8 * SIZE + (slots if h == JOINED else 0)
-        step = 256
+        step = 512
 
         def one(j, carry):
             cols = pl.ds(pl.multiple_of(j * step, step), step)

time: 69 us -> 66.8 us (0.968)
  Pallas kernels: 67.4 us -> 65.2 us
    pallas_call x1, Pallas kernels: 65.6 us -> 63.3 us  [on_device(): pl.pallas_call(functools.partial(layer_kernel, groups), name='layer', out...]
where the time goes in v5:
time: 66.8 us; the launch traced here: 66.6 us
  Pallas kernels  65.2 us (98%)
  between operations  1.45 us (2%)
    pallas_call x1, Pallas kernels, on_device(): pl.pallas_call(functools.partial(layer_kernel, groups), name='layer', out...  63.3 us
    pallas_call x1, Pallas kernels, on_device(): pl.pallas_call(hand_out, name='hand_out', out_shape=tuple((shape(result.s...  1.88 us

profile of v5, /device:TPU:1, one launch (start us, length us, event | category | flops | bytes accessed | tf_op | source)
XLA Modules:
  0.0 66.6 jit_solution(5172765255947450496)
XLA Ops:
  1.3 63.3 %layer.1 = (bf16[64,2048]{1,0:T(8,128)(2,1)}, bf16[2,2048]{1,0:T(2,128)(2,1)}, bf16[2,512,128]{2,1,0:T(8,128)(2,1)}, bf16[2,16,128]{2,1,0:T(8,128)(2,1)}) custom-call(bf16[64,2048]{1,0:T(8,128)(2,1)} %rows_hbm.1, bf16[2,2048]{1,0:T(2,128)(2,1)} %drows_hbm.1, s32[1,256]{1,0:T(1,128)} %bitcast.7, s32[1]{0:T(128)S(6)} %copy.18.off_hbm, s32[16]{0:T(128)} %len_hbm.1, ...), custom_call_target="tpu_custom_call" | custom-call | tf_op jit(solution)/shard_map/layer/pallas_call | solution.py:791
  64.6 1.9 %hand_out.1 = (bf16[64,2048]{1,0:T(8,128)(2,1)}, bf16[2,2048]{1,0:T(2,128)(2,1)}, bf16[2,512,128]{2,1,0:T(8,128)(2,1)}, bf16[2,16,128]{2,1,0:T(8,128)(2,1)}) custom-call(bf16[64,2048]{1,0:T(8,128)(2,1)} %get-tuple-element.8.refs_0_, bf16[2,2048]{1,0:T(2,128)(2,1)} %get-tuple-element.9.refs_1_, bf16[2,512,128]{2,1,0:T(8,128)(2,1)} %get-tuple-element.10.refs_2_, ...), custom_call_target="tpu_custom_call" | custom-call | tf_op jit(solution)/shard_map/hand_out/pallas_call | solution.py:883
